TPU v7x, 256 devices: a whole 4x4x8 slice. The times are simulated.
256 devices in a mesh: blk: 16 (over y, x_lo, core), rep: 16 (over z, x_hi).
Axes of the slice: x: 4 (x_hi: 2, x_lo: 2; x = x_hi * 2 + x_lo), y: 4, z: 8, core: 2. Of those that a mesh axis runs over, the one named last changes fastest.
Arguments:
- features: bfloat16 [65536, 128], P(('blk', 'rep')), may hold values from -6 to 6
- edge_rows: int32 [16, 16, 32, 256], P('blk', None, 'rep'), may hold values from 0 to 4095
- edge_cols: int32 [16, 16, 32, 256], P('blk', None, 'rep'), may hold values from 0 to 127
- weight: bfloat16 [128, 256], replicated, may hold values from -0.5 to 0.5
- bias: float32 [256], replicated, may hold values from -3 to 3
- upstream: bfloat16 [65536, 256], P('blk'), may hold values from -6 to 6
- train_mask: int32 [65536], P('blk'), may hold values 0 or 1
Outputs:
- activations: bfloat16 [65536, 256], P(('blk', 'rep'))
- grad_features: bfloat16 [65536, 128], P(('blk', 'rep'))
- grad_weight: float32 [128, 256], replicated
- grad_bias: float32 [256], replicated
Inputs may be any that keep to these rules, and one draw needn't show every extreme that they name: `edge_rows`: target indices within a panel. `edge_cols`: source indices within a column block.
All inputs are finite; a program needn't handle non-finite values. No bound on the sum of `train_mask` on one device may be relied on, other than what follows from the above.
Results may differ from a plain program's by a relative error of at most 0.018.
Values may be sent and summed in bfloat16 or wider, within the bound.
No kernel may reach another device: no remote copies, remote signals or barrier semaphores. Data moves between devices by JAX's collectives and lax.ppermute only.
A program may use at most 64 MiB of HBM per device.

v0:
```python
import math

import jax
import jax.numpy as jnp
from jax import lax
from jax.sharding import PartitionSpec as P

CB = 128


def from_everyone(value, axis):
    copies = jnp.broadcast_to(value, (lax.axis_size(axis), *value.shape))
    return lax.all_to_all(copies, axis, split_axis=0, concat_axis=0, tiled=True)


def in_order(parts, dim):
    lengths = list(parts.shape[1:])
    lengths[dim] *= parts.shape[0]
    return jnp.moveaxis(parts, 0, dim).reshape(lengths)


def gathered_copies(value, axis, dim):
    parts = from_everyone(value, axis)
    return in_order(parts, dim)


def in_blocks(value, dim, count):
    lengths = value.shape
    parts = value.reshape(*lengths[:dim], count, lengths[dim] // count, *lengths[dim + 1 :])
    return jnp.moveaxis(parts, dim, 0)


def summed_on_arrival(value, axis, dim):
    parts = in_blocks(value, dim, lax.axis_size(axis))
    arrived = lax.all_to_all(parts, axis, split_axis=0, concat_axis=0, tiled=True)
    return arrived.astype(jnp.float32).sum(axis=0)


def sent_together(arrays, axis, dim, along):
    widths = [math.prod(a.shape[along:]) for a in arrays]
    both = jnp.concatenate(
        [a.reshape(*a.shape[:along], w) for a, w in zip(arrays, widths)], axis=along
    )
    whole = summed_on_arrival(both, axis, dim)
    parts = jnp.split(whole, [sum(widths[:k]) for k in range(1, len(widths))], axis=along)
    return tuple((b.reshape(*whole.shape[:along], *a.shape[along:]) for a, b in zip(arrays, parts)))


def together(arrays, axis):
    ends = [0]
    for a in arrays:
        ends.append(ends[-1] + a.size)
    subtotal = lax.psum(jnp.concatenate([a.ravel() for a in arrays]), axis)
    return tuple((subtotal[b:e].reshape(a.shape) for a, b, e in zip(arrays, ends, ends[1:])))


def dense_layer(feats, gathered, counts, upstream, train_mask, weight, bias):
    degree = 1.0 + counts
    mixed_in = ((feats.astype(jnp.float32) + gathered) / degree[:, None]).astype(jnp.bfloat16)
    pre_act = jnp.dot(mixed_in, weight, preferred_element_type=jnp.float32) + bias
    gate_value = jax.nn.sigmoid(pre_act)
    activations = (pre_act * gate_value).astype(jnp.bfloat16)
    slope = gate_value * (1.0 + pre_act * (1.0 - gate_value))
    grad_pre = (
        upstream.astype(jnp.float32) * train_mask.astype(jnp.float32)[:, None] * slope
    ).astype(jnp.bfloat16)
    scaled_back = (
        jnp.dot(grad_pre, weight.T, preferred_element_type=jnp.float32) / degree[:, None]
    ).astype(jnp.bfloat16)
    return (mixed_in, activations, grad_pre, scaled_back)


def on_device(features, edge_rows, edge_cols, weight, bias, upstream, train_mask):
    piece_rows, feature_width = features.shape
    edge_slots = edge_rows.shape[-1]
    panel_rows = upstream.shape[0]
    flat_rows = edge_rows.reshape(-1, edge_slots)
    flat_cols = edge_cols.reshape(-1, edge_slots)
    rep_index = lax.axis_index("rep")
    counts_part = jnp.zeros((panel_rows,), jnp.float32).at[flat_rows.reshape(-1)].add(1.0)
    shard_rows = gathered_copies(features, "blk", 0)
    block_count = shard_rows.shape[0] // CB
    targets = flat_rows
    columns = flat_cols
    offsets = (jnp.arange(block_count, dtype=jnp.int32) * CB)[:, None]
    values = jnp.take(shard_rows, (offsets + columns).reshape(-1), axis=0).astype(jnp.float32)
    partial_sums = (
        jnp.zeros((panel_rows, feature_width), jnp.float32).at[targets.reshape(-1)].add(values)
    )
    gathered, counts = sent_together(
        (partial_sums.astype(jnp.bfloat16), counts_part.astype(jnp.bfloat16)), "rep", 0, 1
    )
    own_upstream = lax.dynamic_slice_in_dim(upstream, rep_index * piece_rows, piece_rows, 0)
    own_mask = lax.dynamic_slice_in_dim(train_mask, rep_index * piece_rows, piece_rows, 0)
    mixed_own, activations, grad_own, back_own = dense_layer(
        features, gathered, counts, own_upstream, own_mask, weight, bias
    )
    back_panel = gathered_copies(back_own, "rep", 0)
    weight_part = lax.dot_general(
        mixed_own, grad_own, (((0,), (0,)), ((), ())), preferred_element_type=jnp.float32
    )
    bias_part = jnp.sum(grad_own.astype(jnp.float32), axis=0)
    grad_weight, grad_bias = together((weight_part, bias_part), ("blk", "rep"))
    row_count = piece_rows * lax.axis_size("blk")
    block_count = row_count // CB
    targets = flat_rows
    columns = flat_cols
    values = jnp.take(back_panel, targets.reshape(-1), axis=0).reshape(
        block_count, edge_slots, feature_width
    )
    one_hot = (columns[:, :, None] == jnp.arange(CB, dtype=jnp.int32)[None, None, :]).astype(
        jnp.bfloat16
    )
    block_terms = jnp.einsum("nec,ned->ncd", one_hot, values, preferred_element_type=jnp.float32)
    received = summed_on_arrival(
        block_terms.reshape(row_count, feature_width).astype(jnp.bfloat16), "blk", 0
    )
    grad_features = (back_own.astype(jnp.float32) + received).astype(jnp.bfloat16)
    return (activations, grad_features, grad_weight, grad_bias)


def solution(mesh):
    return jax.shard_map(
        on_device,
        mesh=mesh,
        in_specs=(
            P(("blk", "rep"), None),
            P("blk", None, "rep", None),
            P("blk", None, "rep", None),
            P(),
            P(),
            P("blk", None),
            P("blk"),
        ),
        out_specs=(P(("blk", "rep"), None), P(("blk", "rep"), None), P(), P()),
        check_vma=False,
    )
```

profile of v0, /device:TPU:1, one launch (start us, length us, event | category | flops | bytes accessed | tf_op | source)
XLA Modules:
  0.0 513.5 jit_solution(3568390661544370196)
XLA Ops:
  7.2 0.0 copy-start
  7.2 0.0 copy-start.4
  7.2 0.0 copy-start.3
  7.2 2.1 broadcast_in_dim.33
  9.3 6.9 %all-to-all-start = ((bf16[16,256,128]{2,1,0:T(8,128)(2,1)}), bf16[16,256,128]{2,1,0:T(8,128)(2,1)S(1)}, u32[]{:S(2)}, u32[]{:S(2)}) async-start(bf16[16,256,128]{2,1,0:T(8,128)(2,1)} %broadcast_in_dim.33), calls=%async_computation | async-start | bytes 2097152 | tf_op jit(solution)/shard_map/all_to_all | solution.py:13
  16.2 0.0 copy-done.4
  16.2 0.1 reshape_reshape.7
  16.3 0.1 broadcast_bitcast_fusion
  16.4 0.0 copy-done.3
  16.5 43.2 %scatter_custom_fusion.1 = f32[4096]{0:T(1024)S(1)} fusion(s32[8192]{0:T(1024)S(1)} %bitcast.37, f32[8192]{0:T(1024)S(1)} %broadcast.37, f32[]{:T(128)} %constant.15.clone.1), kind=kCustom, calls=%fused_computation.37 | custom fusion | flops 8192 | bytes 16388 | tf_op jit(solution)/shard_map/scatter-add | solution.py:80
  59.7 3.1 concatenate.15
  62.9 0.0 all-to-all-done
  62.9 73.9 %scatter_custom_fusion = f32[4096,128]{1,0:T(8,128)S(1)} fusion(s32[8192]{0:T(1024)S(1)} %bitcast.38, pred[8192]{0:T(1024)(128)(4,1)S(1)} %compare_and_fusion.1, bf16[]{:T(256)} %constant.11.clone.2, f32[]{:T(128)} %constant.15.clone.1, bf16[4096,128]{1,0:T(8,128)(2,1)S(1)} %bitcast.25, s32[8192]{0:T(1024)S(1)} %broadcast_clamp_fusion), kind=kCustom, calls=%fused_computation.5 | custom fusion | flops 3145728 | bytes 3186694 | tf_op jit(solution)/shard_map/scatter-add | solution.py:88
  136.7 0.0 copy-start.1
  136.7 0.1 convert_element_type.55
  136.9 1.1 copy-done.1
  138.0 0.5 pad_maximum_fusion
  138.4 2.2 copy.16
  140.6 10.6 %all-to-all-start.1 = ((bf16[16,256,129]{1,2,0:T(8,128)(2,1)}), bf16[16,256,129]{1,2,0:T(8,128)(2,1)S(1)}, u32[]{:S(2)}, u32[]{:S(2)}) async-start(bf16[16,256,129]{1,2,0:T(8,128)(2,1)} %copy.16), calls=%async_computation.1 | async-start | bytes 2228224 | tf_op jit(solution)/shard_map/all_to_all | solution.py:35
  151.2 0.8 dynamic-slice_convert_fusion
  152.0 27.8 %all-to-all-done.1 = bf16[16,256,129]{1,2,0:T(8,128)(2,1)S(1)} async-done(((bf16[16,256,129]{1,2,0:T(8,128)(2,1)}), bf16[16,256,129]{1,2,0:T(8,128)(2,1)S(1)}, u32[]{:S(2)}, u32[]{:S(2)}) %all-to-all-start.1) | async-done | bytes 1056800 | tf_op jit(solution)/shard_map/all_to_all | solution.py:35
  179.8 0.2 convert_reduce_fusion
  180.0 0.1 copy.18
  180.1 0.0 copy-done.2
  180.1 0.1 divide_convert_fusion
  180.2 1.8 convert_reduce_fusion.2
  182.0 0.2 fusion.7
  182.2 1.2 broadcast_in_dim.36
  183.4 6.0 %all-to-all-start.2 = ((bf16[16,256,128]{2,1,0:T(8,128)(2,1)}), bf16[16,256,128]{2,1,0:T(8,128)(2,1)S(1)}, u32[]{:S(2)}, u32[]{:S(2)}) async-start(bf16[16,256,128]{2,1,0:T(8,128)(2,1)} %broadcast_in_dim.36), calls=%async_computation.2 | async-start | bytes 2097152 | tf_op jit(solution)/shard_map/all_to_all | solution.py:13
  189.4 0.6 eq.15
  190.1 25.4 %all-to-all-done.2 = bf16[16,256,128]{2,1,0:T(8,128)(2,1)S(1)} async-done(((bf16[16,256,128]{2,1,0:T(8,128)(2,1)}), bf16[16,256,128]{2,1,0:T(8,128)(2,1)S(1)}, u32[]{:S(2)}, u32[]{:S(2)}) %all-to-all-start.2) | async-done | bytes 1048608 | tf_op jit(solution)/shard_map/all_to_all | solution.py:13
  215.5 24.0 %gather_fusion = bf16[8192,128]{1,0:T(8,128)(2,1)S(1)} fusion(bf16[4096,128]{1,0:T(8,128)(2,1)S(1)} %bitcast.24, s32[8192]{0:T(1024)S(1)} %fusion.10), kind=kCustom, calls=%fused_computation.1.clone | custom fusion | bytes 4227072 | tf_op jit(solution)/shard_map/jit(_take)/gather | solution.py:108
  239.5 0.0 copy-start.5
  239.5 4.3 broadcast_select_fusion
  243.8 1.9 fusion.6
  245.7 9.6 %all-to-all-start.3 = ((bf16[16,256,128]{2,1,0:T(8,128)(2,1)}), bf16[16,256,128]{2,1,0:T(8,128)(2,1)S(1)}, u32[]{:S(2)}, u32[]{:S(2)}) async-start(bf16[16,256,128]{2,1,0:T(8,128)(2,1)} %bitcast.6), calls=%async_computation.3 | async-start | bytes 2097152 | tf_op jit(solution)/shard_map/all_to_all | solution.py:35
  255.3 0.0 all-reduce.2.cloned.1.call-start
  255.4 0.2 convolution_bitcast_fusion
  255.5 0.1 copy.22
  255.6 0.7 pad_maximum_fusion.1
  256.3 0.0 all-reduce.2.cloned.1.call-update
  256.3 246.7 %all-reduce.2.cloned.1.call-done = f32[33024]{0:T(1024)} async-done(((f32[33024]{0:T(1024)}), f32[33024]{0:T(1024)}) %all-reduce.2.cloned.1.call-update) | async-done | bytes 132112 | tf_op jit(solution)/shard_map/psum | solution.py:53
  503.0 0.9 slice.23
  503.9 0.7 slice.17
  504.6 1.2 slice.24
  505.8 0.0 all-to-all-done.3
  505.8 0.1 convert_reduce_fusion.1
  506.0 0.6 add_convert_fusion
  (18 shorter events, 0.2 us)
Async XLA Ops:
  7.2 173.0 %copy-start = (bf16[128,256]{1,0:T(8,128)(2,1)S(1)}, bf16[128,256]{1,0:T(8,128)(2,1)}, u32[]{:S(2)}) copy-start(bf16[128,256]{1,0:T(8,128)(2,1)} %param.12) | copy-start | bytes 196612
  7.2 9.0 %copy-start.4 = (s32[1,16,2,256]{3,2,1,0:T(2,128)S(1)}, s32[1,16,2,256]{3,2,1,0:T(2,128)}, u32[]{:S(2)}) copy-start(s32[1,16,2,256]{3,2,1,0:T(2,128)} %param.10) | copy-start | bytes 98308
  7.2 9.2 %copy-start.3 = (s32[1,16,2,256]{3,2,1,0:T(2,128)S(1)}, s32[1,16,2,256]{3,2,1,0:T(2,128)}, u32[]{:S(2)}) copy-start(s32[1,16,2,256]{3,2,1,0:T(2,128)} %param.11) | copy-start | bytes 98308
  9.3 53.6 %all-to-all-start = ((bf16[16,256,128]{2,1,0:T(8,128)(2,1)}), bf16[16,256,128]{2,1,0:T(8,128)(2,1)S(1)}, u32[]{:S(2)}, u32[]{:S(2)}) async-start(bf16[16,256,128]{2,1,0:T(8,128)(2,1)} %broadcast_in_dim.33), calls=%async_computation | async-start | bytes 2097152 | tf_op jit(solution)/shard_map/all_to_all | solution.py:13
  136.7 1.2 copy-start.1
  140.6 39.5 %copy-start.2 = (bf16[256,128]{1,0:T(8,128)(2,1)S(1)}, bf16[256,128]{1,0:T(8,128)(2,1)}, u32[]{:S(2)}) copy-start(bf16[256,128]{1,0:T(8,128)(2,1)} %param.9) | copy-start | bytes 196612
  140.6 39.6 %copy-start.6 = (f32[256]{0:T(256)S(1)}, f32[256]{0:T(256)}, u32[]{:S(2)}) copy-start(f32[256]{0:T(256)} %param.13) | copy-start | bytes 3076
  140.6 39.2 %all-to-all-start.1 = ((bf16[16,256,129]{1,2,0:T(8,128)(2,1)}), bf16[16,256,129]{1,2,0:T(8,128)(2,1)S(1)}, u32[]{:S(2)}, u32[]{:S(2)}) async-start(bf16[16,256,129]{1,2,0:T(8,128)(2,1)} %copy.16), calls=%async_computation.1 | async-start | bytes 2228224 | tf_op jit(solution)/shard_map/all_to_all | solution.py:35
  183.4 32.1 %all-to-all-start.2 = ((bf16[16,256,128]{2,1,0:T(8,128)(2,1)}), bf16[16,256,128]{2,1,0:T(8,128)(2,1)S(1)}, u32[]{:S(2)}, u32[]{:S(2)}) async-start(bf16[16,256,128]{2,1,0:T(8,128)(2,1)} %broadcast_in_dim.36), calls=%async_computation.2 | async-start | bytes 2097152 | tf_op jit(solution)/shard_map/all_to_all | solution.py:13
  239.5 4.3 copy-start.5
  245.7 260.2 %all-to-all-start.3 = ((bf16[16,256,128]{2,1,0:T(8,128)(2,1)}), bf16[16,256,128]{2,1,0:T(8,128)(2,1)S(1)}, u32[]{:S(2)}, u32[]{:S(2)}) async-start(bf16[16,256,128]{2,1,0:T(8,128)(2,1)} %bitcast.6), calls=%async_computation.3 | async-start | bytes 2097152 | tf_op jit(solution)/shard_map/all_to_all | solution.py:35
  255.3 247.7 %all-reduce.2.cloned.1.call-start = ((), (), s32[]{:S(2)}) async-start(), calls=%async_computation.4 | async-start | bytes 270336 | tf_op jit(solution)/shard_map/psum | solution.py:53
Sparse Core Ops, SparseCore 0:
  261.6 241.3 all-reduce.1
where the time goes:
time: 514 us; the launch traced here: 513 us
  waiting for transfers between devices  300 us (58%)
  other arithmetic  124 us (24%)
  local copies, waits for them, and re-layouts  37.6 us (7%)
  starting transfers between devices  33.1 us (6%)
  between operations  14.3 us (3%)
    psum x1, waiting for transfers between devices, together(): subtotal = lax.psum(jnp.concatenate([a.ravel() for a in arrays]), axis)  247 us
    scatter-add x1, other arithmetic, on_device(): jnp.zeros((panel_rows, feature_width), jnp.float32).at[targets.reshape(-1)]  73.9 us
    scatter-add x1, other arithmetic, on_device(): jnp.zeros((panel_rows,), jnp.float32).at[flat_rows.reshape(-1)].add(1.0)  43.2 us
    all_to_all x2, waiting for transfers between devices, summed_on_arrival(): lax.all_to_all(parts, axis, split_axis=0, concat_axis=0, tiled=True)  27.8 us
    all_to_all x2, waiting for transfers between devices, from_everyone(): return lax.all_to_all(copies, axis, split_axis=0, concat_axis=0, tiled=True)  25.4 us
    gather x1, local copies, waits for them, and re-layouts, on_device(): jnp.take(back_panel, targets.reshape(-1), axis=0)  24 us
    all_to_all x2, starting transfers between devices, summed_on_arrival(): lax.all_to_all(parts, axis, split_axis=0, concat_axis=0, tiled=True)  20.2 us
    all_to_all x2, starting transfers between devices, from_everyone(): return lax.all_to_all(copies, axis, split_axis=0, concat_axis=0, tiled=True)  12.9 us
  transfers between devices with their start and end apart: 5, of which 3 were waited for; matrix products, arithmetic and copies ran while one was open for 10% of the time, Pallas kernels for 0%

commit v1 on v0

v1 whole, which is shorter than its diff:
```python
import functools

import jax
import jax.numpy as jnp
from jax import lax
from jax.experimental import pallas as pl
from jax.experimental.pallas import tpu as pltpu
from jax.sharding import PartitionSpec as P

CB = 128
LANES = 128
BF = jnp.bfloat16
F32 = jnp.float32
TN = (((0,), (0,)), ((), ()))
NT = (((1,), (1,)), ((), ()))
ACCS = 4
UNROLL = 16

VMEM = pl.BlockSpec(memory_space=pltpu.VMEM)
SMEM = pl.BlockSpec(memory_space=pltpu.SMEM)


def exchange(parts, axis):
    return lax.all_to_all(parts, axis, split_axis=0, concat_axis=0, tiled=True)


def from_everyone(value, axis):
    return exchange(jnp.broadcast_to(value, (lax.axis_size(axis), *value.shape)), axis)


def one_hot(index, count):
    hits = lax.broadcasted_iota(jnp.int32, (count, index.shape[-1]), 0) == index
    return hits.astype(F32).astype(BF)


def count_kernel(rows_ref, out_ref):
    rows = rows_ref[...]
    total = jnp.zeros(out_ref.shape, F32)
    for k in range(rows.shape[0]):
        index = rows[k : k + 1, :]
        high = one_hot(jnp.right_shift(index, 7), out_ref.shape[0])
        low = one_hot(jnp.bitwise_and(index, LANES - 1), LANES)
        total += lax.dot_general(high, low, NT, preferred_element_type=F32)
    out_ref[...] = total


def gather_sum_kernel(rows_ref, sources_ref, table_ref, counts_ref, out_ref, wide_ref, *totals):
    pieces = out_ref.shape[0]
    piece_rows = wide_ref.shape[0] // pieces
    edges = rows_ref.shape[0] * rows_ref.shape[1]
    wide_ref[...] = table_ref[...].astype(F32)
    for total in totals:
        total[...] = jnp.zeros_like(total)

    @pl.loop(0, rows_ref.shape[0])
    def _(i):
        for u in range(0, UNROLL, ACCS):
            rows = [rows_ref[i, u + j] for j in range(ACCS)]
            values = [wide_ref[pl.ds(sources_ref[i, u + j], 1), :] for j in range(ACCS)]
            olds = [totals[j][pl.ds(rows[j], 1), :] for j in range(ACCS)]
            for j in range(ACCS):
                totals[j][pl.ds(rows[j], 1), :] = olds[j] + values[j]

    @pl.loop(0, pieces)
    def _(p):
        span = pl.ds(p * piece_rows, piece_rows)
        part = totals[0][span, :]
        for total in totals[1:]:
            part += total[span, :]
        out_ref[p, :piece_rows, :] = part.astype(BF)
        groups = piece_rows // LANES
        count = counts_ref[pl.ds(p * groups, groups), :]
        high = jnp.floor(count * (1.0 / 128.0))
        low = count - high * 128.0
        rest = jnp.zeros((8 - 2 * groups, LANES), F32)
        out_ref[p, piece_rows:, :] = jnp.concatenate([high, low, rest], 0).astype(BF)


def spread_kernel(rows_ref, cols_ref, table_ref, out_ref, wide_ref, picked_ref):
    wide_ref[...] = table_ref[...].astype(F32)
    slots = cols_ref.shape[1]
    steps = slots // UNROLL

    @pl.loop(0, cols_ref.shape[0])
    def _(k):
        @pl.loop(0, steps)
        def _(i):
            for u in range(UNROLL):
                picked_ref[pl.ds(i * UNROLL + u, 1), :] = wide_ref[
                    pl.ds(rows_ref[k * steps + i, u], 1), :
                ]

        hits = one_hot(cols_ref[pl.ds(k, 1), :], CB)
        terms = jnp.dot(hits, picked_ref[...].astype(BF), preferred_element_type=F32)
        out_ref[pl.ds(pl.multiple_of(k * CB, CB), CB), :] = terms.astype(BF)


def as_column(row):
    size = row.shape[1]
    diagonal = lax.broadcasted_iota(jnp.int32, (size, size), 0) == lax.broadcasted_iota(
        jnp.int32, (size, size), 1
    )
    return jnp.sum(jnp.where(diagonal, row, 0.0), axis=1, keepdims=True)


def dense_kernel(
    place_ref, parts_ref, feats_ref, upstream_ref, mask_ref, weight_ref, bias_ref,
    act_ref, back_ref, wpart_ref, bpart_ref,
):
    piece_rows, width = feats_ref.shape
    total = parts_ref[0].astype(F32)
    for p in range(1, parts_ref.shape[0]):
        total += parts_ref[p].astype(F32)
    groups = piece_rows // LANES
    counts = total[piece_rows : piece_rows + groups] * 128.0 + total[
        piece_rows + groups : piece_rows + 2 * groups
    ]
    degree = 1.0 + jnp.concatenate([as_column(counts[g : g + 1]) for g in range(groups)], 0)
    mask = jnp.concatenate([as_column(mask_ref[g : g + 1].astype(F32)) for g in range(groups)], 0)
    mixed = ((feats_ref[...].astype(F32) + total[:piece_rows]) / degree).astype(BF)
    weight = weight_ref[...]
    pre = jnp.dot(mixed, weight, preferred_element_type=F32) + bias_ref[...]
    gate = 1.0 / (1.0 + jnp.exp(-pre))
    act_ref[...] = (pre * gate).astype(BF)
    slope = gate * (1.0 + pre * (1.0 - gate))
    grad = (upstream_ref[...].astype(F32) * mask * slope).astype(BF)
    back = lax.dot_general(grad, weight, NT, preferred_element_type=F32) / degree
    back_ref[...] = back.astype(BF)
    wpart_ref[...] = lax.dot_general(mixed, grad, TN, preferred_element_type=F32)
    bpart_ref[...] = jnp.sum(grad.astype(F32), axis=0, keepdims=True)


def close_kernel(terms_ref, back_ref, out_ref):
    total = back_ref[...].astype(F32)
    for p in range(terms_ref.shape[0]):
        total += terms_ref[p].astype(F32)
    out_ref[...] = total.astype(BF)


def on_device(features, edge_rows, edge_cols, weight, bias, upstream, train_mask):
    piece_rows, width = features.shape
    hidden = weight.shape[1]
    slots = edge_rows.shape[-1]
    panel_rows = upstream.shape[0]
    n_blk, n_rep = lax.axis_size("blk"), lax.axis_size("rep")
    place = lax.axis_index("rep")
    rows = edge_rows.reshape(-1, slots)
    cols = edge_cols.reshape(-1, slots)
    blocks = rows.shape[0]
    edges = blocks * slots

    table = from_everyone(features, "blk").reshape(n_blk * piece_rows, width)
    counts = pl.pallas_call(
        count_kernel,
        in_specs=[VMEM],
        out_specs=VMEM,
        out_shape=jax.ShapeDtypeStruct((panel_rows // LANES, LANES), F32),
        name="count",
    )(rows)
    sources = cols + (jnp.arange(blocks, dtype=jnp.int32) * CB)[:, None]
    row_list = rows.reshape(-1, UNROLL)
    source_list = sources.reshape(-1, UNROLL)

    sends = pl.pallas_call(
        gather_sum_kernel,
        in_specs=[SMEM, SMEM, VMEM, VMEM],
        out_specs=VMEM,
        out_shape=jax.ShapeDtypeStruct((n_rep, piece_rows + 8, width), BF),
        scratch_shapes=[pltpu.VMEM((panel_rows, width), F32)] * (ACCS + 1),
        name="gather_sum",
    )(row_list, source_list, table, counts)
    parts = exchange(sends, "rep")

    activations, back, weight_part, bias_part = pl.pallas_call(
        dense_kernel,
        grid_spec=pltpu.PrefetchScalarGridSpec(
            num_scalar_prefetch=1,
            grid=(1,),
            in_specs=[
                pl.BlockSpec(parts.shape, lambda i, s: (0, 0, 0)),
                pl.BlockSpec(features.shape, lambda i, s: (0, 0)),
                pl.BlockSpec((piece_rows, hidden), lambda i, s: (s[0], 0)),
                pl.BlockSpec((None, piece_rows // LANES, LANES), lambda i, s: (s[0], 0, 0)),
                pl.BlockSpec(weight.shape, lambda i, s: (0, 0)),
                pl.BlockSpec((1, hidden), lambda i, s: (0, 0)),
            ],
            out_specs=[
                pl.BlockSpec((piece_rows, hidden), lambda i, s: (0, 0)),
                pl.BlockSpec((piece_rows, width), lambda i, s: (0, 0)),
                pl.BlockSpec((width, hidden), lambda i, s: (0, 0)),
                pl.BlockSpec((1, hidden), lambda i, s: (0, 0)),
            ],
        ),
        out_shape=[
            jax.ShapeDtypeStruct((piece_rows, hidden), BF),
            jax.ShapeDtypeStruct((piece_rows, width), BF),
            jax.ShapeDtypeStruct((width, hidden), F32),
            jax.ShapeDtypeStruct((1, hidden), F32),
        ],
        name="dense",
    )(
        place.astype(jnp.int32).reshape(1),
        parts,
        features,
        upstream,
        train_mask.reshape(n_rep, piece_rows // LANES, LANES),
        weight,
        bias.reshape(1, hidden),
    )

    back_panel = from_everyone(back, "rep").reshape(panel_rows, width)

    share = width // n_blk
    slim = hidden // n_blk
    both = jnp.concatenate(
        [
            weight_part.reshape(n_blk, share * hidden // LANES, LANES),
            jnp.pad(bias_part.reshape(n_blk, 1, slim), ((0, 0), (0, 7), (0, LANES - slim))),
        ],
        axis=1,
    )
    mine = jnp.sum(exchange(both, "blk"), axis=0)
    mine = jnp.sum(from_everyone(mine, "rep"), axis=0)
    whole = from_everyone(mine, "blk")
    grad_weight = whole[:, : share * hidden // LANES].reshape(width, hidden)
    grad_bias = whole[:, share * hidden // LANES, :slim].reshape(hidden)

    terms = pl.pallas_call(
        spread_kernel,
        in_specs=[SMEM, VMEM, VMEM],
        out_specs=VMEM,
        out_shape=jax.ShapeDtypeStruct((n_blk * piece_rows, width), BF),
        scratch_shapes=[pltpu.VMEM((panel_rows, width), F32), pltpu.VMEM((slots, width), F32)],
        name="spread",
    )(row_list, cols, back_panel)
    received = exchange(terms.reshape(n_blk, piece_rows, width), "blk")
    grad_features = pl.pallas_call(
        close_kernel,
        in_specs=[VMEM, VMEM],
        out_specs=VMEM,
        out_shape=jax.ShapeDtypeStruct((piece_rows, width), BF),
        name="close",
    )(received, back)
    return (activations, grad_features, grad_weight, grad_bias)


def solution(mesh):
    return jax.shard_map(
        on_device,
        mesh=mesh,
        in_specs=(
            P(("blk", "rep"), None),
            P("blk", None, "rep", None),
            P("blk", None, "rep", None),
            P(),
            P(),
            P("blk", None),
            P("blk"),
        ),
        out_specs=(P(("blk", "rep"), None), P(("blk", "rep"), None), P(), P()),
        check_vma=False,
    )
```

time: 514 us -> 210 us (0.41)
  waiting for transfers between devices: 300 us -> 78.1 us
  other arithmetic: 124 us -> 2.24 us
  Pallas kernels: 0 us -> 52.8 us
  blocking collectives: 0 us -> 27.2 us
  local copies, waits for them, and re-layouts: 37.6 us -> 12.2 us
  between operations: 14.3 us -> 0.72 us
    psum x1 -> x0, waiting for transfers between devices: 247 us -> none  [together(): subtotal = lax.psum(jnp.concatenate([a.ravel() for a in arrays]), axis)]
    scatter-add x2 -> x0, other arithmetic: 117 us -> none  [the longest x1 73.9 us: on_device(): jnp.zeros((panel_rows, feature_width), jnp.float32).at[targets.reshape(-1)]]
    pallas_call x0 -> x5, Pallas kernels: none -> 52.8 us  [the longest x1 26 us: on_device(): pl.pallas_call(gather_sum_kernel, in_specs=[SMEM, SMEM, VMEM, VMEM], out_...]
    all_to_all x0 -> x2, blocking collectives: none -> 27.2 us  [exchange(): return lax.all_to_all(parts, axis, split_axis=0, concat_axis=0, tiled=True)]
    all_to_all x4 -> x5, waiting for transfers between devices: 53.2 us -> 78.1 us  [exchange(): return lax.all_to_all(parts, axis, split_axis=0, concat_axis=0, tiled=True)]
    gather x1 -> x0, local copies, waits for them, and re-layouts: 24 us -> none  [on_device(): jnp.take(back_panel, targets.reshape(-1), axis=0)]
    concatenate x2 -> x0, local copies, waits for them, and re-layouts: 5.28 us -> none  [sent_together(): jnp.concatenate([a.reshape(*a.shape[:along], w) for a, w in zip(arrays, w...]
    all_to_all x4 -> x5, starting transfers between devices: 33.1 us -> 35.6 us  [exchange(): return lax.all_to_all(parts, axis, split_axis=0, concat_axis=0, tiled=True)]
  transfers between devices with their start and end apart: 5 -> 5, of which waited for: 3 -> 4; matrix products, arithmetic and copies ran while one was open for 10% -> 2% of each run, Pallas kernels for 0% -> 11%
where the time goes in v1:
time: 210 us; the launch traced here: 209 us
  waiting for transfers between devices  78.1 us (37%)
  Pallas kernels  52.8 us (25%)
  starting transfers between devices  35.6 us (17%)
  blocking collectives  27.2 us (13%)
  local copies, waits for them, and re-layouts  12.2 us (6%)
  other arithmetic  2.24 us (1%)
    all_to_all x5, waiting for transfers between devices, exchange(): return lax.all_to_all(parts, axis, split_axis=0, concat_axis=0, tiled=True)  78.1 us
    all_to_all x5, starting transfers between devices, exchange(): return lax.all_to_all(parts, axis, split_axis=0, concat_axis=0, tiled=True)  35.6 us
    all_to_all x2, blocking collectives, exchange(): return lax.all_to_all(parts, axis, split_axis=0, concat_axis=0, tiled=True)  27.2 us
    pallas_call x1, Pallas kernels, on_device(): pl.pallas_call(gather_sum_kernel, in_specs=[SMEM, SMEM, VMEM, VMEM], out_...  26 us
    pallas_call x1, Pallas kernels, on_device(): pl.pallas_call(spread_kernel, in_specs=[SMEM, VMEM, VMEM], out_specs=VMEM...  20 us
  transfers between devices with their start and end apart: 5, of which 4 were waited for; matrix products, arithmetic and copies ran while one was open for 2% of the time, Pallas kernels for 11%

profile of v1, /device:TPU:1, one launch (start us, length us, event | category | flops | bytes accessed | tf_op | source)
XLA Modules:
  0.0 208.9 jit_solution(1304783125896517025)
XLA Ops:
  0.6 2.0 broadcast_in_dim.13
  2.6 0.0 copy-start.5
  2.6 0.0 copy-start.6
  2.6 7.0 %all-to-all-start = ((bf16[16,256,128]{2,1,0:T(8,128)(2,1)}), bf16[16,256,128]{2,1,0:T(8,128)(2,1)S(1)}, u32[]{:S(2)}, u32[]{:S(2)}) async-start(bf16[16,256,128]{2,1,0:T(8,128)(2,1)} %broadcast_in_dim.13), calls=%async_computation | async-start | bytes 2097152 | tf_op jit(solution)/shard_map/all_to_all | solution.py:24
  9.7 0.0 copy-done.5
  9.7 0.9 reshape_reshape.3.rows_ref
  10.5 0.6 reshape.53.rows_ref
  11.2 0.0 copy-done.6
  11.2 0.1 reshape.51
  11.3 0.1 add.15
  11.4 0.1 add.16
  11.5 2.2 %count.1.counts_ref = f32[32,128]{1,0:T(8,128)} custom-call(s32[32,256]{1,0:T(8,128)} %reshape.53.rows_ref), custom_call_target="tpu_custom_call" | custom-call | tf_op jit(solution)/shard_map/count/pallas_call | solution.py:153
  13.7 0.8 broadcast_add_fusion.sources_ref
  14.5 10.8 %all-to-all-done = bf16[16,256,128]{2,1,0:T(8,128)(2,1)S(1)} async-done(((bf16[16,256,128]{2,1,0:T(8,128)(2,1)}), bf16[16,256,128]{2,1,0:T(8,128)(2,1)S(1)}, u32[]{:S(2)}, u32[]{:S(2)}) %all-to-all-start) | async-done | bytes 1048608 | tf_op jit(solution)/shard_map/all_to_all | solution.py:24
  25.3 0.0 copy-start.3
  25.3 1.0 copy-done.3
  26.4 26.0 %gather_sum.1 = bf16[16,264,128]{2,1,0:T(8,128)(2,1)} custom-call(s32[512,16]{1,0:T(8,128)} %reshape_reshape.3.rows_ref, s32[512,16]{1,0:T(8,128)} %broadcast_add_fusion.sources_ref, bf16[4096,128]{1,0:T(8,128)(2,1)} %bitcast.9, f32[32,128]{1,0:T(8,128)} %count.1.counts_ref), custom_call_target="tpu_custom_call" | custom-call | tf_op jit(solution)/shard_map/gather_sum/pallas_call | solution.py:164
  52.4 10.5 %all-to-all-start.1 = ((bf16[16,264,128]{2,1,0:T(8,128)(2,1)}), bf16[16,264,128]{2,1,0:T(8,128)(2,1)S(1)}, u32[]{:S(2)}, u32[]{:S(2)}) async-start(bf16[16,264,128]{2,1,0:T(8,128)(2,1)} %gather_sum.1), calls=%async_computation.1 | async-start | bytes 2162688 | tf_op jit(solution)/shard_map/all_to_all | solution.py:24
  62.8 27.2 %all-to-all-done.1.parts_ref = bf16[16,264,128]{2,1,0:T(8,128)(2,1)S(1)} async-done(((bf16[16,264,128]{2,1,0:T(8,128)(2,1)}), bf16[16,264,128]{2,1,0:T(8,128)(2,1)S(1)}, u32[]{:S(2)}, u32[]{:S(2)}) %all-to-all-start.1) | async-done | bytes 1081376 | tf_op jit(solution)/shard_map/all_to_all | solution.py:24
  90.0 0.0 copy-start
  90.0 1.0 copy-done
  91.0 2.6 %dense.1 = (bf16[256,256]{1,0:T(8,128)(2,1)}, bf16[256,128]{1,0:T(8,128)(2,1)}, f32[128,256]{1,0:T(8,128)}, f32[1,256]{1,0:T(1,128)}) custom-call(s32[1]{0:T(128)} %bitcast.place_ref, bf16[16,264,128]{2,1,0:T(8,128)(2,1)} %copy-done, bf16[256,128]{1,0:T(8,128)(2,1)} %feats_ref.1, bf16[4096,256]{1,0:T(8,128)(2,1)} %upstream_ref.1, s32[16,2,128]{2,1,0:T(2,128)} %bitcast.11, ...), custom_call_target="tpu_custom_call" | custom-call | tf_op jit(solution)/shard_map/dense/pallas_call | solution.py:174
  93.6 0.0 copy-start.4
  93.6 0.9 reshape.59
  94.5 0.5 broadcast.18
  95.1 1.3 reduce.7
  96.4 0.1 reshape.60
  96.5 13.6 %all_to_all.35 = f32[16,24,128]{2,1,0:T(8,128)S(1)} all-to-all(f32[16,24,128]{2,1,0:T(8,128)S(1)} %select_maximum_fusion), channel_id=1, replica_groups=mesh['blk'=16,'rep'=16] {'blk'}, dimensions={0} | all-to-all | bytes 393216 | tf_op jit(solution)/shard_map/all_to_all | solution.py:24
  110.1 13.6 %all_to_all.36 = f32[16,24,128]{2,1,0:T(8,128)S(1)} all-to-all(f32[16,24,128]{2,1,0:T(8,128)S(1)} %broadcast_in_dim.15), channel_id=1, replica_groups=mesh['blk'=16,'rep'=16] {'rep'}, dimensions={0} | all-to-all | bytes 393216 | tf_op jit(solution)/shard_map/all_to_all | solution.py:24
  123.7 0.0 copy-done.4
  123.7 1.2 broadcast_in_dim.14
  124.9 3.7 %all-to-all-start.2 = ((bf16[16,256,128]{2,1,0:T(8,128)(2,1)}), bf16[16,256,128]{2,1,0:T(8,128)(2,1)S(1)}, u32[]{:S(2)}, u32[]{:S(2)}) async-start(bf16[16,256,128]{2,1,0:T(8,128)(2,1)} %broadcast_in_dim.14), calls=%async_computation.2 | async-start | bytes 2097152 | tf_op jit(solution)/shard_map/all_to_all | solution.py:24
  128.6 25.9 %all-to-all-done.2 = bf16[16,256,128]{2,1,0:T(8,128)(2,1)S(1)} async-done(((bf16[16,256,128]{2,1,0:T(8,128)(2,1)}), bf16[16,256,128]{2,1,0:T(8,128)(2,1)S(1)}, u32[]{:S(2)}, u32[]{:S(2)}) %all-to-all-start.2) | async-done | bytes 1048608 | tf_op jit(solution)/shard_map/all_to_all | solution.py:24
  154.4 0.0 copy-start.1
  154.4 0.7 broadcast_in_dim.16
  155.2 8.7 %all-to-all-start.6 = ((f32[16,24,128]{2,1,0:T(8,128)}), f32[16,24,128]{2,1,0:T(8,128)S(1)}, u32[]{:S(2)}, u32[]{:S(2)}) async-start(f32[16,24,128]{2,1,0:T(8,128)} %broadcast_in_dim.16), calls=%async_computation.6 | async-start | bytes 393216 | tf_op jit(solution)/shard_map/all_to_all | solution.py:24
  163.8 0.6 reshape.56.cols_ref
  164.5 0.0 copy-done.1
  164.5 20.0 %spread.1 = bf16[4096,128]{1,0:T(8,128)(2,1)} custom-call(s32[512,16]{1,0:T(8,128)} %reshape_reshape.3.rows_ref, s32[32,256]{1,0:T(8,128)} %reshape.56.cols_ref, bf16[4096,128]{1,0:T(8,128)(2,1)} %bitcast.7), custom_call_target="tpu_custom_call" | custom-call | tf_op jit(solution)/shard_map/spread/pallas_call | solution.py:228
  184.5 0.0 all-to-all-done.6
  184.5 5.8 %all-to-all-start.3 = ((bf16[16,256,128]{2,1,0:T(8,128)(2,1)}), bf16[16,256,128]{2,1,0:T(8,128)(2,1)S(1)}, u32[]{:S(2)}, u32[]{:S(2)}) async-start(bf16[16,256,128]{2,1,0:T(8,128)(2,1)} %bitcast.8), calls=%async_computation.3 | async-start | bytes 2097152 | tf_op jit(solution)/shard_map/all_to_all | solution.py:24
  190.3 0.7 reshape.61
  191.0 0.6 reshape_squeeze.3
  191.7 14.3 %all-to-all-done.3.terms_ref = bf16[16,256,128]{2,1,0:T(8,128)(2,1)S(1)} async-done(((bf16[16,256,128]{2,1,0:T(8,128)(2,1)}), bf16[16,256,128]{2,1,0:T(8,128)(2,1)S(1)}, u32[]{:S(2)}, u32[]{:S(2)}) %all-to-all-start.3) | async-done | bytes 1048608 | tf_op jit(solution)/shard_map/all_to_all | solution.py:24
  205.9 0.0 copy-start.2
  205.9 1.0 copy-done.2
  206.9 2.0 close.1
  (7 shorter events, 0.1 us)
Async XLA Ops:
  2.6 7.0 %copy-start.5 = (s32[1,16,2,256]{3,2,1,0:T(2,128)S(1)}, s32[1,16,2,256]{3,2,1,0:T(2,128)}, u32[]{:S(2)}) copy-start(s32[1,16,2,256]{3,2,1,0:T(2,128)} %param.8) | copy-start | bytes 98308
  2.6 8.5 %copy-start.6 = (s32[1,16,2,256]{3,2,1,0:T(2,128)S(1)}, s32[1,16,2,256]{3,2,1,0:T(2,128)}, u32[]{:S(2)}) copy-start(s32[1,16,2,256]{3,2,1,0:T(2,128)} %param.9) | copy-start | bytes 98308
  2.6 22.7 %all-to-all-start = ((bf16[16,256,128]{2,1,0:T(8,128)(2,1)}), bf16[16,256,128]{2,1,0:T(8,128)(2,1)S(1)}, u32[]{:S(2)}, u32[]{:S(2)}) async-start(bf16[16,256,128]{2,1,0:T(8,128)(2,1)} %broadcast_in_dim.13), calls=%async_computation | async-start | bytes 2097152 | tf_op jit(solution)/shard_map/all_to_all | solution.py:24
  25.3 1.0 copy-start.3
  52.4 37.6 %all-to-all-start.1 = ((bf16[16,264,128]{2,1,0:T(8,128)(2,1)}), bf16[16,264,128]{2,1,0:T(8,128)(2,1)S(1)}, u32[]{:S(2)}, u32[]{:S(2)}) async-start(bf16[16,264,128]{2,1,0:T(8,128)(2,1)} %gather_sum.1), calls=%async_computation.1 | async-start | bytes 2162688 | tf_op jit(solution)/shard_map/all_to_all | solution.py:24
  90.0 1.0 copy-start
  93.6 30.1 %copy-start.4 = (bf16[256,128]{1,0:T(8,128)(2,1)S(1)}, bf16[256,128]{1,0:T(8,128)(2,1)}, u32[]{:S(2)}) copy-start(bf16[256,128]{1,0:T(8,128)(2,1)} %get-tuple-element.9.back_ref) | copy-start | bytes 196612
  124.9 29.5 %all-to-all-start.2 = ((bf16[16,256,128]{2,1,0:T(8,128)(2,1)}), bf16[16,256,128]{2,1,0:T(8,128)(2,1)S(1)}, u32[]{:S(2)}, u32[]{:S(2)}) async-start(bf16[16,256,128]{2,1,0:T(8,128)(2,1)} %broadcast_in_dim.14), calls=%async_computation.2 | async-start | bytes 2097152 | tf_op jit(solution)/shard_map/all_to_all | solution.py:24
  154.4 10.0 %copy-start.1 = (bf16[16,256,128]{2,1,0:T(8,128)(2,1)}, bf16[16,256,128]{2,1,0:T(8,128)(2,1)S(1)}, u32[]{:S(2)}) copy-start(bf16[16,256,128]{2,1,0:T(8,128)(2,1)S(1)} %all-to-all-done.2) | copy-start | bytes 3145732
  155.2 29.4 %all-to-all-start.6 = ((f32[16,24,128]{2,1,0:T(8,128)}), f32[16,24,128]{2,1,0:T(8,128)S(1)}, u32[]{:S(2)}, u32[]{:S(2)}) async-start(f32[16,24,128]{2,1,0:T(8,128)} %broadcast_in_dim.16), calls=%async_computation.6 | async-start | bytes 393216 | tf_op jit(solution)/shard_map/all_to_all | solution.py:24
  184.5 21.4 %all-to-all-start.3 = ((bf16[16,256,128]{2,1,0:T(8,128)(2,1)}), bf16[16,256,128]{2,1,0:T(8,128)(2,1)S(1)}, u32[]{:S(2)}, u32[]{:S(2)}) async-start(bf16[16,256,128]{2,1,0:T(8,128)(2,1)} %bitcast.8), calls=%async_computation.3 | async-start | bytes 2097152 | tf_op jit(solution)/shard_map/all_to_all | solution.py:24
  205.9 1.0 copy-start.2

commit v2 on v1

v2 whole, which is shorter than its diff:
```python
import jax
import jax.numpy as jnp
from jax import lax
from jax.experimental import pallas as pl
from jax.experimental.pallas import tpu as pltpu
from jax.sharding import PartitionSpec as P


CB = 128
LANES = 128
BF = jnp.bfloat16
F32 = jnp.float32
TN = (((0,), (0,)), ((), ()))
NT = (((1,), (1,)), ((), ()))
TOTALS = 8
CHUNK = 1024

VMEM = pl.BlockSpec(memory_space=pltpu.VMEM)
ANY = pl.BlockSpec(memory_space=pl.ANY)


def cost(us):
    return pl.CostEstimate(flops=0, transcendentals=0, bytes_accessed=int(us * 3.0e6))


def exchange(parts, axis):
    return lax.all_to_all(parts, axis, split_axis=0, concat_axis=0, tiled=True)


def from_everyone(value, axis):
    return exchange(jnp.broadcast_to(value, (lax.axis_size(axis), *value.shape)), axis)


def one_hot(index, count):
    hits = lax.broadcasted_iota(jnp.int32, (count, index.shape[-1]), 0) == index
    return hits.astype(F32).astype(BF)


def count_kernel(rows_ref, out_ref):
    rows = rows_ref[...]
    total = jnp.zeros(out_ref.shape, F32)
    for k in range(rows.shape[0]):
        index = rows[k : k + 1, :]
        high = one_hot(jnp.right_shift(index, 7), out_ref.shape[0])
        low = one_hot(jnp.bitwise_and(index, LANES - 1), LANES)
        total += lax.dot_general(high, low, NT, preferred_element_type=F32)
    out_ref[...] = total


def gather_sum_kernel(
    rows_ref, cols_ref, table_ref, counts_ref, out_ref, list0, list1, sems, values0, values1, *totals
):
    lists, values = (list0, list1), (values0, values1)
    pieces = out_ref.shape[0]
    piece_rows = totals[0].shape[0] // pieces
    blocks, slots = cols_ref.shape
    held = CHUNK // slots
    steps = blocks // held // 2

    def fetch(step, side):
        return pltpu.make_async_copy(rows_ref.at[pl.ds(step * CHUNK, CHUNK)], lists[side], sems.at[side])

    def pick(k, side):
        hits = one_hot(cols_ref[pl.ds(k, 1), :], CB)
        block = table_ref[pl.ds(pl.multiple_of(k * CB, CB), CB), :]
        values[side][...] = lax.dot_general(hits, block, TN, preferred_element_type=F32)

    for side in range(2):
        fetch(side, side).start()
    for total in totals:
        total[...] = jnp.zeros_like(total)
    pick(0, 0)

    @pl.loop(0, steps)
    def _(i):
        for side in range(2):
            fetch(2 * i + side, side).wait()
            for s in range(held):
                pick(jnp.minimum((2 * i + side) * held + s + 1, blocks - 1), (s + 1) % 2)
                for u in range(0, slots, TOTALS):
                    rows = [lists[side][s * slots + u + j] for j in range(TOTALS)]
                    olds = [totals[j][pl.ds(rows[j], 1), :] for j in range(TOTALS)]
                    for j in range(TOTALS):
                        new = olds[j] + values[s % 2][u + j : u + j + 1, :]
                        totals[j][pl.ds(rows[j], 1), :] = new

            @pl.when(i < steps - 1)
            def _():
                fetch(2 * i + side + 2, side).start()

    @pl.loop(0, pieces)
    def _(p):
        span = pl.ds(p * piece_rows, piece_rows)
        part = totals[0][span, :]
        for total in totals[1:]:
            part += total[span, :]
        out_ref[p, :piece_rows, :] = part.astype(BF)
        groups = piece_rows // LANES
        count = counts_ref[pl.ds(p * groups, groups), :]
        high = jnp.floor(count * (1.0 / 128.0))
        low = count - high * 128.0
        rest = jnp.zeros((8 - 2 * groups, LANES), F32)
        out_ref[p, piece_rows:, :] = jnp.concatenate([high, low, rest], 0).astype(BF)


def spread_kernel(rows_ref, cols_ref, table_ref, out_ref, list0, list1, sems, wide_ref, picked0, picked1):
    lists, picked = (list0, list1), (picked0, picked1)
    pieces = table_ref.shape[0]
    piece_rows = wide_ref.shape[0] // pieces
    blocks, slots = cols_ref.shape
    held = CHUNK // slots
    steps = blocks // held // 2

    def fetch(step, side):
        return pltpu.make_async_copy(rows_ref.at[pl.ds(step * CHUNK, CHUNK)], lists[side], sems.at[side])

    for side in range(2):
        fetch(side, side).start()
    for p in range(pieces):
        wide_ref[p * piece_rows : (p + 1) * piece_rows, :] = table_ref[p, :piece_rows, :].astype(F32)

    @pl.loop(0, steps)
    def _(i):
        for side in range(2):
            fetch(2 * i + side, side).wait()
            for s in range(held):
                k = (2 * i + side) * held + s
                for u in range(slots):
                    row = wide_ref[pl.ds(lists[side][s * slots + u], 1), :]
                    picked[s % 2][u : u + 1, :] = row
                hits = one_hot(cols_ref[pl.ds(k, 1), :], CB)
                terms = jnp.dot(hits, picked[s % 2][...].astype(BF), preferred_element_type=F32)
                out_ref[pl.ds(pl.multiple_of(k * CB, CB), CB), :] = terms.astype(BF)

            @pl.when(i < steps - 1)
            def _():
                fetch(2 * i + side + 2, side).start()


def as_column(row):
    size = row.shape[1]
    diagonal = lax.broadcasted_iota(jnp.int32, (size, size), 0) == lax.broadcasted_iota(
        jnp.int32, (size, size), 1
    )
    return jnp.sum(jnp.where(diagonal, row, 0.0), axis=1, keepdims=True)


def dense_kernel(
    place_ref, parts_ref, feats_ref, upstream_ref, mask_ref, weight_ref, bias_ref,
    act_ref, back_ref, sends_ref,
):
    piece_rows, width = feats_ref.shape
    total = parts_ref[0].astype(F32)
    for p in range(1, parts_ref.shape[0]):
        total += parts_ref[p].astype(F32)
    groups = piece_rows // LANES
    counts = total[piece_rows : piece_rows + groups] * 128.0 + total[
        piece_rows + groups : piece_rows + 2 * groups
    ]
    degree = 1.0 + jnp.concatenate([as_column(counts[g : g + 1]) for g in range(groups)], 0)
    mask = jnp.concatenate([as_column(mask_ref[g : g + 1].astype(F32)) for g in range(groups)], 0)
    mixed = ((feats_ref[...].astype(F32) + total[:piece_rows]) / degree).astype(BF)
    weight = weight_ref[...]
    pre = jnp.dot(mixed, weight, preferred_element_type=F32) + bias_ref[...]
    gate = 1.0 / (1.0 + jnp.exp(-pre))
    act_ref[...] = (pre * gate).astype(BF)
    slope = gate * (1.0 + pre * (1.0 - gate))
    grad = (upstream_ref[...].astype(F32) * mask * slope).astype(BF)
    back = lax.dot_general(grad, weight, NT, preferred_element_type=F32) / degree
    back = back.astype(BF)
    back_ref[...] = back
    weight_part = lax.dot_general(mixed, grad, TN, preferred_element_type=F32).astype(BF)
    bias_part = jnp.sum(grad.astype(F32), axis=0, keepdims=True)
    spans = range(0, bias_part.shape[1], LANES)
    rest = jnp.zeros((8 - len(spans), LANES), F32)
    bias_part = jnp.concatenate([bias_part[:, c : c + LANES] for c in spans] + [rest], 0).astype(BF)
    share = width // sends_ref.shape[0]
    for p in range(sends_ref.shape[0]):
        pieces = [weight_part[p * share : (p + 1) * share, c : c + LANES] for c in spans]
        sends_ref[p] = jnp.concatenate([back, *pieces, bias_part], 0)


def close_kernel(terms_ref, back_ref, out_ref):
    total = back_ref[...].astype(F32)
    for p in range(terms_ref.shape[0]):
        total += terms_ref[p].astype(F32)
    out_ref[...] = total.astype(BF)


def layer(features, edge_rows, edge_cols, weight, bias, upstream, train_mask):
    piece_rows, width = features.shape
    hidden = weight.shape[1]
    slots = edge_rows.shape[-1]
    panel_rows = upstream.shape[0]
    n_blk, n_rep = lax.axis_size("blk"), lax.axis_size("rep")
    place = lax.axis_index("rep")
    rows = edge_rows.reshape(-1, slots)
    cols = edge_cols.reshape(-1, slots)

    table = from_everyone(features, "blk").reshape(n_blk * piece_rows, width)
    counts = pl.pallas_call(
        count_kernel,
        in_specs=[VMEM],
        out_specs=VMEM,
        out_shape=jax.ShapeDtypeStruct((panel_rows // LANES, LANES), F32),
        cost_estimate=cost(2),
        name="count",
    )(rows)
    row_list = rows.reshape(-1)
    chunks = [pltpu.SMEM((CHUNK,), jnp.int32)] * 2 + [pltpu.SemaphoreType.DMA((2,))]

    sends = pl.pallas_call(
        gather_sum_kernel,
        in_specs=[ANY, VMEM, VMEM, VMEM],
        out_specs=VMEM,
        out_shape=jax.ShapeDtypeStruct((n_rep, piece_rows + 8, width), BF),
        scratch_shapes=chunks
        + [pltpu.VMEM((slots, width), F32)] * 2
        + [pltpu.VMEM((panel_rows, width), F32)] * TOTALS,
        cost_estimate=cost(14),
        name="gather_sum",
    )(row_list, cols, table, counts)
    parts = exchange(sends, "rep")

    share = width // n_rep
    spans = hidden // LANES
    extra = share * spans + 8
    activations, back, sends = pl.pallas_call(
        dense_kernel,
        grid_spec=pltpu.PrefetchScalarGridSpec(
            num_scalar_prefetch=1,
            grid=(1,),
            in_specs=[
                pl.BlockSpec(parts.shape, lambda i, s: (0, 0, 0)),
                pl.BlockSpec(features.shape, lambda i, s: (0, 0)),
                pl.BlockSpec((piece_rows, hidden), lambda i, s: (s[0], 0)),
                pl.BlockSpec((None, piece_rows // LANES, LANES), lambda i, s: (s[0], 0, 0)),
                pl.BlockSpec(weight.shape, lambda i, s: (0, 0)),
                pl.BlockSpec((1, hidden), lambda i, s: (0, 0)),
            ],
            out_specs=[
                pl.BlockSpec((piece_rows, hidden), lambda i, s: (0, 0)),
                pl.BlockSpec((piece_rows, width), lambda i, s: (0, 0)),
                pl.BlockSpec((n_rep, piece_rows + extra, width), lambda i, s: (0, 0, 0)),
            ],
        ),
        out_shape=[
            jax.ShapeDtypeStruct((piece_rows, hidden), BF),
            jax.ShapeDtypeStruct((piece_rows, width), BF),
            jax.ShapeDtypeStruct((n_rep, piece_rows + extra, width), BF),
        ],
        cost_estimate=cost(3),
        name="dense",
    )(
        place.astype(jnp.int32).reshape(1),
        parts,
        features,
        upstream,
        train_mask.reshape(n_rep, piece_rows // LANES, LANES),
        weight,
        bias.reshape(1, hidden),
    )

    panel = exchange(sends, "rep")

    mine = jnp.sum(panel[:, piece_rows:].astype(F32), axis=0)
    arrived = from_everyone(mine, "blk")
    terms = pl.pallas_call(
        spread_kernel,
        in_specs=[ANY, VMEM, VMEM],
        out_specs=VMEM,
        out_shape=jax.ShapeDtypeStruct((n_blk * piece_rows, width), BF),
        scratch_shapes=chunks
        + [pltpu.VMEM((panel_rows, width), F32)]
        + [pltpu.VMEM((slots, width), F32)] * 2,
        cost_estimate=cost(14),
        name="spread",
    )(row_list, cols, panel)
    terms, arrived = lax.optimization_barrier((terms, arrived))
    received = exchange(terms.reshape(n_blk, piece_rows, width), "blk")
    mine = jnp.sum(arrived, axis=0)
    grad_bias = mine[share * spans : share * spans + spans].reshape(hidden)
    whole = mine[: share * spans][None]
    for bit in (8, 4, 1, 2):
        theirs = lax.ppermute(whole, "rep", [(i, i ^ bit) for i in range(n_rep)])
        upper = jnp.bitwise_and(place, bit) != 0
        whole = jnp.stack([jnp.where(upper, theirs, whole), jnp.where(upper, whole, theirs)], 0)
        whole = whole.reshape(-1, share * spans, LANES)
    whole = whole.reshape(2, 2, 2, 2, spans, share, LANES)
    whole = whole.transpose(3, 2, 0, 1, 5, 4, 6)
    grad_weight = whole.reshape(width, hidden)

    grad_features = pl.pallas_call(
        close_kernel,
        in_specs=[VMEM, VMEM],
        out_specs=VMEM,
        out_shape=jax.ShapeDtypeStruct((piece_rows, width), BF),
        cost_estimate=cost(1),
        name="close",
    )(received, back)
    return (activations, grad_features, grad_weight, grad_bias)


def solution(mesh):
    return jax.shard_map(
        layer,
        mesh=mesh,
        in_specs=(
            P(("blk", "rep"), None),
            P("blk", None, "rep", None),
            P("blk", None, "rep", None),
            P(),
            P(),
            P("blk", None),
            P("blk"),
        ),
        out_specs=(P(("blk", "rep"), None), P(("blk", "rep"), None), P(), P()),
        check_vma=False,
    )
```

time: 210 us -> 170 us (0.81)
  Pallas kernels: 52.8 us -> 27.6 us
  waiting for transfers between devices: 78.1 us -> 60.3 us
  blocking collectives: 27.2 us -> 38.5 us
  starting transfers between devices: 35.6 us -> 31.9 us
  local copies, waits for them, and re-layouts: 12.2 us -> 8.87 us
  other arithmetic: 2.24 us -> 0.1 us
    all_to_all x5 -> x4, waiting for transfers between devices: 78.1 us -> 38.8 us  [exchange(): return lax.all_to_all(parts, axis, split_axis=0, concat_axis=0, tiled=True)]
    pallas_call x5, Pallas kernels: 52.8 us -> 27.6 us  [the longest x1 10.3 us: layer(): pl.pallas_call(gather_sum_kernel, in_specs=[ANY, VMEM, VMEM, VMEM], out_s...]
    ppermute x0 -> x4, waiting for transfers between devices: none -> 21.5 us  [layer(): theirs = lax.ppermute(whole, 'rep', [(i, i ^ bit) for i in range(n_rep)])]
    all_to_all x2 -> x1, blocking collectives: 27.2 us -> 38.5 us  [exchange(): return lax.all_to_all(parts, axis, split_axis=0, concat_axis=0, tiled=True)]
    all_to_all x5 -> x4, starting transfers between devices: 35.6 us -> 30.1 us  [exchange(): return lax.all_to_all(parts, axis, split_axis=0, concat_axis=0, tiled=True)]
  transfers between devices with their start and end apart: 5 -> 8, of which waited for: 4 -> 5; matrix products, arithmetic and copies ran while one was open for 2% -> 2% of each run, Pallas kernels for 11% -> 7%
where the time goes in v2:
time: 170 us; the launch traced here: 168 us
  waiting for transfers between devices  60.3 us (35%)
  blocking collectives  38.5 us (23%)
  starting transfers between devices  31.9 us (19%)
  Pallas kernels  27.6 us (16%)
  local copies, waits for them, and re-layouts  8.87 us (5%)
    all_to_all x4, waiting for transfers between devices, exchange(): return lax.all_to_all(parts, axis, split_axis=0, concat_axis=0, tiled=True)  38.8 us
    all_to_all x1, blocking collectives, exchange(): return lax.all_to_all(parts, axis, split_axis=0, concat_axis=0, tiled=True)  38.5 us
    all_to_all x4, starting transfers between devices, exchange(): return lax.all_to_all(parts, axis, split_axis=0, concat_axis=0, tiled=True)  30.1 us
    ppermute x4, waiting for transfers between devices, layer(): theirs = lax.ppermute(whole, 'rep', [(i, i ^ bit) for i in range(n_rep)])  21.5 us
    pallas_call x1, Pallas kernels, layer(): pl.pallas_call(gather_sum_kernel, in_specs=[ANY, VMEM, VMEM, VMEM], out_s...  10.3 us
    pallas_call x1, Pallas kernels, layer(): pl.pallas_call(spread_kernel, in_specs=[ANY, VMEM, VMEM], out_specs=VMEM,...  10.2 us
    unnamed x13, local copies, waits for them, and re-layouts  3.6 us
  transfers between devices with their start and end apart: 8, of which 5 were waited for; matrix products, arithmetic and copies ran while one was open for 2% of the time, Pallas kernels for 7%

profile of v2, /device:TPU:1, one launch (start us, length us, event | category | flops | bytes accessed | tf_op | source)
XLA Modules:
  0.0 168.0 jit_solution(9813663240286596622)
XLA Ops:
  0.6 2.0 %broadcast_in_dim.9 = bf16[16,256,128]{2,1,0:T(8,128)(2,1)} broadcast(bf16[256,128]{1,0:T(8,128)(2,1)} %feats_ref.1), dimensions={1,2} | broadcast | bytes 1114112 | tf_op jit(solution)/shard_map/broadcast_in_dim | solution.py:31
  2.7 0.0 copy-start.4
  2.7 0.0 copy-start.5
  2.7 7.0 %all-to-all-start = ((bf16[16,256,128]{2,1,0:T(8,128)(2,1)}), bf16[16,256,128]{2,1,0:T(8,128)(2,1)S(1)}, u32[]{:S(2)}, u32[]{:S(2)}) async-start(bf16[16,256,128]{2,1,0:T(8,128)(2,1)} %broadcast_in_dim.9), calls=%async_computation | async-start | bytes 2097152 | tf_op jit(solution)/shard_map/all_to_all | solution.py:27
  9.7 0.0 copy-done.4
  9.7 0.6 reshape.51.rows_ref
  10.3 0.6 copy.15
  11.0 0.0 copy-done.5
  11.0 0.6 reshape.49.cols_ref
  11.6 2.2 %count.1.counts_ref = f32[32,128]{1,0:T(8,128)} custom-call(s32[32,256]{1,0:T(8,128)} %reshape.51.rows_ref), custom_call_target="tpu_custom_call" | custom-call | bytes 6000000 | tf_op jit(solution)/shard_map/count/pallas_call | solution.py:201
  13.8 11.6 %all-to-all-done = bf16[16,256,128]{2,1,0:T(8,128)(2,1)S(1)} async-done(((bf16[16,256,128]{2,1,0:T(8,128)(2,1)}), bf16[16,256,128]{2,1,0:T(8,128)(2,1)S(1)}, u32[]{:S(2)}, u32[]{:S(2)}) %all-to-all-start) | async-done | bytes 1048608 | tf_op jit(solution)/shard_map/all_to_all | solution.py:27
  25.4 0.0 copy-start.3
  25.4 1.0 copy-done.3
  26.3 10.3 %gather_sum.1 = bf16[16,264,128]{2,1,0:T(8,128)(2,1)} custom-call(s32[8192]{0:T(1024)} %bitcast.48, s32[32,256]{1,0:T(8,128)} %reshape.49.cols_ref, bf16[4096,128]{1,0:T(8,128)(2,1)} %bitcast.47, f32[32,128]{1,0:T(8,128)} %count.1.counts_ref), custom_call_target="tpu_custom_call" | custom-call | bytes 42000000 | tf_op jit(solution)/shard_map/gather_sum/pallas_call | solution.py:212
  36.7 10.5 %all-to-all-start.1 = ((bf16[16,264,128]{2,1,0:T(8,128)(2,1)}), bf16[16,264,128]{2,1,0:T(8,128)(2,1)S(1)}, u32[]{:S(2)}, u32[]{:S(2)}) async-start(bf16[16,264,128]{2,1,0:T(8,128)(2,1)} %gather_sum.1), calls=%async_computation.1 | async-start | bytes 2162688 | tf_op jit(solution)/shard_map/all_to_all | solution.py:27
  47.1 27.2 %all-to-all-done.1.parts_ref = bf16[16,264,128]{2,1,0:T(8,128)(2,1)S(1)} async-done(((bf16[16,264,128]{2,1,0:T(8,128)(2,1)}), bf16[16,264,128]{2,1,0:T(8,128)(2,1)S(1)}, u32[]{:S(2)}, u32[]{:S(2)}) %all-to-all-start.1) | async-done | bytes 1081376 | tf_op jit(solution)/shard_map/all_to_all | solution.py:27
  74.3 0.0 copy-start.1
  74.3 1.0 copy-done.1
  75.3 3.0 %dense.1 = (bf16[256,256]{1,0:T(8,128)(2,1)}, bf16[256,128]{1,0:T(8,128)(2,1)}, bf16[16,280,128]{2,1,0:T(8,128)(2,1)}) custom-call(s32[1]{0:T(128)} %bitcast.place_ref, bf16[16,264,128]{2,1,0:T(8,128)(2,1)} %copy-done.1, bf16[256,128]{1,0:T(8,128)(2,1)} %feats_ref.1, bf16[4096,256]{1,0:T(8,128)(2,1)} %upstream_ref.1, s32[16,2,128]{2,1,0:T(2,128)} %bitcast.56, ...), custom_call_target="tpu_custom_call" | custom-call | bytes 9000000 | tf_op jit(solution)/shard_map/dense/pallas_call | solution.py:228
  78.3 38.5 %all_to_all.25.table_ref = bf16[16,280,128]{2,1,0:T(8,128)(2,1)S(1)} all-to-all(bf16[16,280,128]{2,1,0:T(8,128)(2,1)} %get-tuple-element.10), channel_id=1, replica_groups=mesh['blk'=16,'rep'=16] {'rep'}, dimensions={0} | all-to-all | bytes 2293760 | tf_op jit(solution)/shard_map/all_to_all | solution.py:27
  116.7 0.0 copy-start
  116.8 0.7 broadcast_in_dim.10
  117.5 5.4 %all-to-all-start.3 = ((f32[16,24,128]{2,1,0:T(8,128)}), f32[16,24,128]{2,1,0:T(8,128)S(1)}, u32[]{:S(2)}, u32[]{:S(2)}) async-start(f32[16,24,128]{2,1,0:T(8,128)} %broadcast_in_dim.10), calls=%async_computation.3 | async-start | bytes 393216 | tf_op jit(solution)/shard_map/all_to_all | solution.py:27
  122.9 0.0 copy-done
  122.9 10.2 %spread.1 = bf16[4096,128]{1,0:T(8,128)(2,1)} custom-call(s32[8192]{0:T(1024)} %bitcast.49, s32[32,256]{1,0:T(8,128)} %reshape.49.cols_ref, bf16[16,280,128]{2,1,0:T(8,128)(2,1)} %copy-done), custom_call_target="tpu_custom_call" | custom-call | bytes 42000000 | tf_op jit(solution)/shard_map/spread/pallas_call | solution.py:268
  133.1 0.0 all-to-all-done.3
  133.1 0.6 collective-permute-start
  133.7 5.9 %collective-permute-done = f32[1,16,128]{2,1,0:T(8,128)S(1)} collective-permute-done((f32[1,16,128]{2,1,0:T(8,128)S(1)}, f32[1,16,128]{2,1,0:T(8,128)S(1)}, u32[]{:S(2)}, u32[]{:S(2)}) %collective-permute-start) | collective-permute-done | bytes 8224 | tf_op jit(solution)/shard_map/ppermute | solution.py:285
  139.7 0.4 collective-permute-start.1
  140.0 7.2 %all-to-all-start.4 = ((bf16[16,256,128]{2,1,0:T(8,128)(2,1)}), bf16[16,256,128]{2,1,0:T(8,128)(2,1)S(1)}, u32[]{:S(2)}, u32[]{:S(2)}) async-start(bf16[16,256,128]{2,1,0:T(8,128)(2,1)} %bitcast.46), calls=%async_computation.4 | async-start | bytes 2097152 | tf_op jit(solution)/shard_map/all_to_all | solution.py:27
  147.2 0.0 collective-permute-done.1
  147.3 0.4 collective-permute-start.2
  147.6 13.4 %collective-permute-done.2 = f32[4,16,128]{2,1,0:T(8,128)S(1)} collective-permute-done((f32[4,16,128]{2,1,0:T(8,128)S(1)}, f32[4,16,128]{2,1,0:T(8,128)S(1)}, u32[]{:S(2)}, u32[]{:S(2)}) %collective-permute-start.2) | collective-permute-done | bytes 32800 | tf_op jit(solution)/shard_map/ppermute | solution.py:285
  161.1 0.5 collective-permute-start.3
  161.6 0.6 slice_bitcast_fusion.1
  162.2 2.1 %collective-permute-done.3 = f32[8,16,128]{2,1,0:T(8,128)S(1)} collective-permute-done((f32[8,16,128]{2,1,0:T(8,128)S(1)}, f32[8,16,128]{2,1,0:T(8,128)S(1)}, u32[]{:S(2)}, u32[]{:S(2)}) %collective-permute-start.3) | collective-permute-done | bytes 65568 | tf_op jit(solution)/shard_map/ppermute | solution.py:285
  164.3 0.7 copy.14
  165.0 0.0 all-to-all-done.4.terms_ref
  165.0 0.0 copy-start.2
  165.0 1.0 copy-done.2
  166.0 2.0 %close.1 = bf16[256,128]{1,0:T(8,128)(2,1)} custom-call(bf16[16,256,128]{2,1,0:T(8,128)(2,1)} %copy-done.2, bf16[256,128]{1,0:T(8,128)(2,1)} %get-tuple-element.12.back_ref), custom_call_target="tpu_custom_call" | custom-call | bytes 3000000 | tf_op jit(solution)/shard_map/close/pallas_call | solution.py:293
  (11 shorter events, 0.1 us)
Async XLA Ops:
  2.7 7.0 %copy-start.4 = (s32[1,16,2,256]{3,2,1,0:T(2,128)S(1)}, s32[1,16,2,256]{3,2,1,0:T(2,128)}, u32[]{:S(2)}) copy-start(s32[1,16,2,256]{3,2,1,0:T(2,128)} %param.8) | copy-start | bytes 98308
  2.7 8.3 %copy-start.5 = (s32[1,16,2,256]{3,2,1,0:T(2,128)S(1)}, s32[1,16,2,256]{3,2,1,0:T(2,128)}, u32[]{:S(2)}) copy-start(s32[1,16,2,256]{3,2,1,0:T(2,128)} %param.9) | copy-start | bytes 98308
  2.7 22.7 %all-to-all-start = ((bf16[16,256,128]{2,1,0:T(8,128)(2,1)}), bf16[16,256,128]{2,1,0:T(8,128)(2,1)S(1)}, u32[]{:S(2)}, u32[]{:S(2)}) async-start(bf16[16,256,128]{2,1,0:T(8,128)(2,1)} %broadcast_in_dim.9), calls=%async_computation | async-start | bytes 2097152 | tf_op jit(solution)/shard_map/all_to_all | solution.py:27
  25.4 1.0 copy-start.3
  36.7 37.7 %all-to-all-start.1 = ((bf16[16,264,128]{2,1,0:T(8,128)(2,1)}), bf16[16,264,128]{2,1,0:T(8,128)(2,1)S(1)}, u32[]{:S(2)}, u32[]{:S(2)}) async-start(bf16[16,264,128]{2,1,0:T(8,128)(2,1)} %gather_sum.1), calls=%async_computation.1 | async-start | bytes 2162688 | tf_op jit(solution)/shard_map/all_to_all | solution.py:27
  74.3 1.0 copy-start.1
  116.7 6.2 %copy-start = (bf16[16,280,128]{2,1,0:T(8,128)(2,1)}, bf16[16,280,128]{2,1,0:T(8,128)(2,1)S(1)}, u32[]{:S(2)}) copy-start(bf16[16,280,128]{2,1,0:T(8,128)(2,1)S(1)} %all_to_all.25.table_ref) | copy-start | bytes 3440644
  117.5 15.6 %all-to-all-start.3 = ((f32[16,24,128]{2,1,0:T(8,128)}), f32[16,24,128]{2,1,0:T(8,128)S(1)}, u32[]{:S(2)}, u32[]{:S(2)}) async-start(f32[16,24,128]{2,1,0:T(8,128)} %broadcast_in_dim.10), calls=%async_computation.3 | async-start | bytes 393216 | tf_op jit(solution)/shard_map/all_to_all | solution.py:27
  133.1 6.5 %collective-permute-start = (f32[1,16,128]{2,1,0:T(8,128)S(1)}, f32[1,16,128]{2,1,0:T(8,128)S(1)}, u32[]{:S(2)}, u32[]{:S(2)}) collective-permute-start(f32[1,16,128]{2,1,0:T(8,128)S(1)} %slice_bitcast_fusion), channel_id=1, source_target_pairs={{0,8},{1,9},{2,10},{3,11},{4,12},{5,13},{6,14},{7,15},{8,0},{9,1},... | collective-permute-start | bytes 24584 | tf_op jit(solution)/shard_map/ppermute | solution.py:285
  139.7 7.6 %collective-permute-start.1 = (f32[2,16,128]{2,1,0:T(8,128)S(1)}, f32[2,16,128]{2,1,0:T(8,128)S(1)}, u32[]{:S(2)}, u32[]{:S(2)}) collective-permute-start(f32[2,16,128]{2,1,0:T(8,128)S(1)} %maximum_bitcast_fusion.1), channel_id=1, source_target_pairs={{0,4},{1,5},{2,6},{3,7},{4,0},{5,1},{6,2},{7,3},{8,12},{9,13},{10,... | collective-permute-start | bytes 49160 | tf_op jit(solution)/shard_map/ppermute | solution.py:285
  140.0 25.0 %all-to-all-start.4 = ((bf16[16,256,128]{2,1,0:T(8,128)(2,1)}), bf16[16,256,128]{2,1,0:T(8,128)(2,1)S(1)}, u32[]{:S(2)}, u32[]{:S(2)}) async-start(bf16[16,256,128]{2,1,0:T(8,128)(2,1)} %bitcast.46), calls=%async_computation.4 | async-start | bytes 2097152 | tf_op jit(solution)/shard_map/all_to_all | solution.py:27
  147.3 13.8 %collective-permute-start.2 = (f32[4,16,128]{2,1,0:T(8,128)S(1)}, f32[4,16,128]{2,1,0:T(8,128)S(1)}, u32[]{:S(2)}, u32[]{:S(2)}) collective-permute-start(f32[4,16,128]{2,1,0:T(8,128)S(1)} %bitcast.55), channel_id=1, source_target_pairs={{0,1},{1,0},{2,3},{3,2},{4,5},{5,4},{6,7},{7,6},{8,9},{9,8},{10,11... | collective-permute-start | bytes 98312 | tf_op jit(solution)/shard_map/ppermute | solution.py:285
  161.1 3.2 %collective-permute-start.3 = (f32[8,16,128]{2,1,0:T(8,128)S(1)}, f32[8,16,128]{2,1,0:T(8,128)S(1)}, u32[]{:S(2)}, u32[]{:S(2)}) collective-permute-start(f32[8,16,128]{2,1,0:T(8,128)S(1)} %bitcast.50), channel_id=1, source_target_pairs={{0,2},{1,3},{2,0},{3,1},{4,6},{5,7},{6,4},{7,5},{8,10},{9,11},{10,... | collective-permute-start | bytes 196616 | tf_op jit(solution)/shard_map/ppermute | solution.py:285
  165.0 1.0 copy-start.2

commit v3 on v2

v3 whole, which is shorter than its diff:
```python
import functools

import jax
import jax.numpy as jnp
from jax import lax
from jax.experimental import pallas as pl
from jax.experimental.pallas import tpu as pltpu
from jax.sharding import PartitionSpec as P


CB = 128
LANES = 128
HALF = 64
BF = jnp.bfloat16
F32 = jnp.float32
TN = (((0,), (0,)), ((), ()))
NT = (((1,), (1,)), ((), ()))
TOTALS = 8
CHUNK = 1024

VMEM = pl.BlockSpec(memory_space=pltpu.VMEM)
ANY = pl.BlockSpec(memory_space=pl.ANY)
SMEM = pl.BlockSpec(memory_space=pltpu.SMEM)


def cost(us):
    return pl.CostEstimate(flops=0, transcendentals=0, bytes_accessed=int(us * 3.0e6))


def exchange(parts, axis, groups=None):
    return lax.all_to_all(
        parts, axis, split_axis=0, concat_axis=0, tiled=True, axis_index_groups=groups
    )


def swapped(value, axis, count, bits):
    return lax.ppermute(value, axis, [(i, i ^ bits) for i in range(count)])


def one_hot(index, count):
    hits = lax.broadcasted_iota(jnp.int32, (count, index.shape[-1]), 0) == index
    return hits.astype(F32).astype(BF)


def turned(value):
    return pltpu.roll(value, HALF, 1)


def left_lanes(rows):
    return lax.broadcasted_iota(jnp.int32, (rows, LANES), 1) < HALF


def unpacked(first, second):
    left = left_lanes(first.shape[0])
    top = jnp.where(left, first, turned(second))
    bottom = jnp.where(left, turned(first), second)
    return jnp.concatenate([top, bottom], 0)


def packed(rows):
    half = rows.shape[0] // 2
    left = left_lanes(half)
    top, bottom = rows[:half], rows[half:]
    return jnp.where(left, top, turned(bottom)), jnp.where(left, turned(top), bottom)


def count_kernel(rows_ref, out_ref):
    rows = rows_ref[...]
    total = jnp.zeros(out_ref.shape, F32)
    for k in range(rows.shape[0]):
        index = rows[k : k + 1, :]
        high = one_hot(jnp.right_shift(index, 7), out_ref.shape[0])
        low = one_hot(jnp.bitwise_and(index, LANES - 1), LANES)
        total += lax.dot_general(high, low, NT, preferred_element_type=F32)
    out_ref[...] = total


def gather_sum_kernel(closing, place_ref, rows_ref, cols_ref, table_ref, *refs):
    if closing:
        counts_ref, before_ref, out_ref, list0, list1, sems, values0, values1, held_ref, sem = refs[:10]
        totals = refs[10:]
        pltpu.make_async_copy(before_ref, held_ref, sem).start()
    else:
        out_ref, list0, list1, sems, values0, values1 = refs[:6]
        totals = refs[6:]
    lists, values = (list0, list1), (values0, values1)
    slots = cols_ref.shape[1]
    blocks = cols_ref.shape[0] // 2
    held = CHUNK // slots
    steps = blocks // held // 2
    core = jnp.bitwise_and(place_ref[1], 1)
    base = (1 - core if closing else core) * blocks

    def fetch(step, side):
        start = pl.multiple_of(base * slots + step * CHUNK, CHUNK)
        return pltpu.make_async_copy(rows_ref.at[pl.ds(start, CHUNK)], lists[side], sems.at[side])

    keep = left_lanes(CB).astype(F32).astype(BF)
    keeps = (keep, 1.0 - keep)

    def pick(k, side):
        hits = one_hot(cols_ref[pl.ds(base + k, 1), :], CB)
        block = table_ref[k >> 1] * keeps[side]
        values[side][...] = lax.dot_general(hits, block, TN, preferred_element_type=F32)

    for side in range(2):
        fetch(side, side).start()
    for total in totals:
        total[...] = jnp.zeros_like(total)
    pick(0, 0)

    @pl.loop(0, steps)
    def _(i):
        for side in range(2):
            fetch(2 * i + side, side).wait()
            for s in range(held):
                pick(jnp.minimum((2 * i + side) * held + s + 1, blocks - 1), (s + 1) % 2)
                for u in range(0, slots, TOTALS):
                    rows = [lists[side][s * slots + u + j] for j in range(TOTALS)]
                    olds = [totals[j][pl.ds(rows[j], 1), :] for j in range(TOTALS)]
                    for j in range(TOTALS):
                        new = olds[j] + values[s % 2][u + j : u + j + 1, :]
                        totals[j][pl.ds(rows[j], 1), :] = new

            @pl.when(i < steps - 1)
            def _():
                fetch(2 * i + side + 2, side).start()

    piece_rows = 2 * CB
    left = left_lanes(CB)
    if closing:
        pltpu.make_async_copy(before_ref, held_ref, sem).wait()

    @pl.loop(0, totals[0].shape[0] // piece_rows)
    def _(p):
        span = pl.ds(p * piece_rows, piece_rows)
        part = totals[0][span, :]
        for total in totals[1:]:
            part += total[span, :]
        if not closing:
            out_ref[span, :] = part
            return
        part += held_ref[span, :]
        part += turned(part)
        out_ref[p, :CB, :] = jnp.where(left, part[:CB], part[CB:]).astype(BF)
        groups = piece_rows // LANES
        count = counts_ref[pl.ds(p * groups, groups), :]
        high = jnp.floor(count * (1.0 / 128.0))
        low = count - high * 128.0
        rest = jnp.zeros((8 - 2 * groups, LANES), F32)
        out_ref[p, CB:, :] = jnp.concatenate([high, low, rest], 0).astype(BF)


def spread_kernel(
    own, place_ref, rows_ref, cols_ref, table_ref, out_ref, list0, list1, sems, wide_ref, picked0, picked1
):
    lists, picked = (list0, list1), (picked0, picked1)
    pieces, half = table_ref.shape[0], CB
    slots = cols_ref.shape[1]
    blocks = cols_ref.shape[0] // 2
    held = CHUNK // slots
    steps = blocks // held // 2
    core = jnp.bitwise_and(place_ref[1], 1)
    base = (core if own else 1 - core) * blocks

    def fetch(step, side):
        start = pl.multiple_of(base * slots + step * CHUNK, CHUNK)
        return pltpu.make_async_copy(rows_ref.at[pl.ds(start, CHUNK)], lists[side], sems.at[side])

    for side in range(2):
        fetch(side, side).start()
    for p in range(pieces):
        block = table_ref[p, :half, :].astype(F32)
        wide_ref[p * 2 * half : (p + 1) * 2 * half, :] = unpacked(block, block)
    left = left_lanes(CB)

    @pl.loop(0, steps)
    def _(i):
        for side in range(2):
            fetch(2 * i + side, side).wait()
            terms = [None, None]
            for s in range(held):
                k = (2 * i + side) * held + s
                for u in range(slots):
                    row = wide_ref[pl.ds(lists[side][s * slots + u], 1), :]
                    picked[s % 2][u : u + 1, :] = row
                hits = one_hot(cols_ref[pl.ds(base + k, 1), :], CB)
                terms[s % 2] = jnp.dot(hits, picked[s % 2][...].astype(BF), preferred_element_type=F32)
                if s % 2 == 1:
                    both = jnp.where(left, terms[0], terms[1]).astype(BF)
                    out_ref[k >> 1] = both

            @pl.when(i < steps - 1)
            def _():
                fetch(2 * i + side + 2, side).start()


def as_column(row):
    size = row.shape[1]
    diagonal = lax.broadcasted_iota(jnp.int32, (size, size), 0) == lax.broadcasted_iota(
        jnp.int32, (size, size), 1
    )
    return jnp.sum(jnp.where(diagonal, row, 0.0), axis=1, keepdims=True)


def dense_kernel(
    place_ref, parts_ref, feats_ref, upstream_ref, mask_ref, weight_ref, bias_ref,
    act_ref, back_ref, sends_ref,
):
    piece_rows, width = feats_ref.shape
    half = piece_rows // 2
    sums = [parts_ref[s].astype(F32) for s in range(2)]
    for p in range(2, parts_ref.shape[0]):
        sums[p % 2] += parts_ref[p].astype(F32)
    gathered = unpacked(sums[0][:half], sums[1][:half])
    groups = piece_rows // LANES
    numbers = sums[0][half:] + sums[1][half:]
    counts = numbers[:groups] * 128.0 + numbers[groups : 2 * groups]
    degree = 1.0 + jnp.concatenate([as_column(counts[g : g + 1]) for g in range(groups)], 0)
    mask = jnp.concatenate([as_column(mask_ref[g : g + 1].astype(F32)) for g in range(groups)], 0)
    mixed = ((feats_ref[...].astype(F32) + gathered) / degree).astype(BF)
    weight = weight_ref[...]
    pre = jnp.dot(mixed, weight, preferred_element_type=F32) + bias_ref[...]
    gate = 1.0 / (1.0 + jnp.exp(-pre))
    act_ref[...] = (pre * gate).astype(BF)
    slope = gate * (1.0 + pre * (1.0 - gate))
    grad = (upstream_ref[...].astype(F32) * mask * slope).astype(BF)
    back = lax.dot_general(grad, weight, NT, preferred_element_type=F32) / degree
    back = back.astype(BF)
    back_ref[...] = back
    sides = [side.astype(BF) for side in packed(back.astype(F32))]
    weight_part = lax.dot_general(mixed, grad, TN, preferred_element_type=F32).astype(BF)
    bias_part = jnp.sum(grad.astype(F32), axis=0, keepdims=True)
    spans = range(0, bias_part.shape[1], LANES)
    rest = jnp.zeros((8 - len(spans), LANES), F32)
    bias_part = jnp.concatenate([bias_part[:, c : c + LANES] for c in spans] + [rest], 0).astype(BF)
    share = width // sends_ref.shape[0]
    for p in range(sends_ref.shape[0]):
        pieces = [weight_part[p * share : (p + 1) * share, c : c + LANES] for c in spans]
        sends_ref[p] = jnp.concatenate([sides[p % 2], *pieces, bias_part], 0)


def close_kernel(terms_ref, back_ref, out_ref):
    sums = [terms_ref[s].astype(F32) for s in range(2)]
    for p in range(2, terms_ref.shape[0]):
        sums[p % 2] += terms_ref[p].astype(F32)
    out_ref[...] = (back_ref[...].astype(F32) + unpacked(sums[0], sums[1])).astype(BF)


def layer(features, edge_rows, edge_cols, weight, bias, upstream, train_mask):
    piece_rows, width = features.shape
    hidden = weight.shape[1]
    slots = edge_rows.shape[-1]
    panel_rows = upstream.shape[0]
    half = piece_rows // 2
    n_blk, n_rep = lax.axis_size("blk"), lax.axis_size("rep")
    panel, place = lax.axis_index("blk"), lax.axis_index("rep")
    planes = [
        [(2 * j + core) * n_rep + 2 * z + s for j in range(n_blk // 2) for s in range(2)]
        for core in range(2)
        for z in range(n_rep // 2)
    ]
    own_rows = edge_rows.reshape(-1, slots)

    left, right = features[:half], features[half:]
    sides = [
        jnp.concatenate([left[:, c : c + HALF], right[:, c : c + HALF]], 1) for c in (0, HALF)
    ]
    sides = jnp.broadcast_to(jnp.stack(sides), (n_blk // 2, 2, half, width)).reshape(-1, half, width)
    table = exchange(sides, ("blk", "rep"), planes)

    other_table = swapped(table, "blk", n_blk, 1)

    edges = jnp.bitwise_or(edge_rows[0], jnp.left_shift(edge_cols[0], 16))
    others = swapped(edges, "rep", n_rep, 1)
    second = jnp.bitwise_and(place, 1) == 1
    both = jnp.stack([jnp.where(second, others, edges), jnp.where(second, edges, others)], 1)
    both = both.reshape(-1, 2, *both.shape[1:]).swapaxes(0, 1).reshape(-1, slots)
    rows = jnp.bitwise_and(both, 0xFFFF)
    cols = jnp.right_shift(both, 16)
    row_list = rows.reshape(-1)

    counts = pl.pallas_call(
        count_kernel,
        in_specs=[VMEM],
        out_specs=VMEM,
        out_shape=jax.ShapeDtypeStruct((panel_rows // LANES, LANES), F32),
        cost_estimate=cost(2),
        name="count",
    )(own_rows)
    chunks = [pltpu.SMEM((CHUNK,), jnp.int32)] * 2 + [pltpu.SemaphoreType.DMA((2,))]

    places = jnp.stack([place, panel]).astype(jnp.int32)
    whole_panel = pltpu.VMEM((panel_rows, width), F32)
    values = [pltpu.VMEM((slots, width), F32)] * 2
    partial = pl.pallas_call(
        functools.partial(gather_sum_kernel, False),
        in_specs=[SMEM, ANY, VMEM, VMEM],
        out_specs=VMEM,
        out_shape=jax.ShapeDtypeStruct((panel_rows, width), F32),
        scratch_shapes=chunks + values + [whole_panel] * TOTALS,
        cost_estimate=cost(10),
        name="gather_own",
    )(places, row_list, cols, table)
    sends = pl.pallas_call(
        functools.partial(gather_sum_kernel, True),
        in_specs=[SMEM, ANY, VMEM, VMEM, VMEM, ANY],
        out_specs=VMEM,
        out_shape=jax.ShapeDtypeStruct((n_rep, half + 8, width), BF),
        scratch_shapes=chunks
        + values
        + [whole_panel, pltpu.SemaphoreType.DMA]
        + [whole_panel] * TOTALS,
        cost_estimate=cost(10),
        name="gather_rest",
    )(places, row_list, cols, other_table, counts, partial)
    parts = exchange(sends, "rep")

    share = width // n_rep
    spans = hidden // LANES
    extra = share * spans + 8
    activations, back, sends = pl.pallas_call(
        dense_kernel,
        grid_spec=pltpu.PrefetchScalarGridSpec(
            num_scalar_prefetch=1,
            grid=(1,),
            in_specs=[
                pl.BlockSpec(parts.shape, lambda i, s: (0, 0, 0)),
                pl.BlockSpec(features.shape, lambda i, s: (0, 0)),
                pl.BlockSpec((piece_rows, hidden), lambda i, s: (s[0], 0)),
                pl.BlockSpec((None, piece_rows // LANES, LANES), lambda i, s: (s[0], 0, 0)),
                pl.BlockSpec(weight.shape, lambda i, s: (0, 0)),
                pl.BlockSpec((1, hidden), lambda i, s: (0, 0)),
            ],
            out_specs=[
                pl.BlockSpec((piece_rows, hidden), lambda i, s: (0, 0)),
                pl.BlockSpec((piece_rows, width), lambda i, s: (0, 0)),
                pl.BlockSpec((n_rep, half + extra, width), lambda i, s: (0, 0, 0)),
            ],
        ),
        out_shape=[
            jax.ShapeDtypeStruct((piece_rows, hidden), BF),
            jax.ShapeDtypeStruct((piece_rows, width), BF),
            jax.ShapeDtypeStruct((n_rep, half + extra, width), BF),
        ],
        cost_estimate=cost(3),
        name="dense",
    )(
        places,
        parts,
        features,
        upstream,
        train_mask.reshape(n_rep, piece_rows // LANES, LANES),
        weight,
        bias.reshape(1, hidden),
    )

    panel_back = exchange(sends, "rep")

    mine = jnp.sum(panel_back[:, half:].astype(F32), axis=0)
    arrived = exchange(jnp.broadcast_to(mine, (n_blk, *mine.shape)), "blk")

    def spread(own):
        return pl.pallas_call(
            functools.partial(spread_kernel, own),
            in_specs=[SMEM, ANY, VMEM, VMEM],
            out_specs=VMEM,
            out_shape=jax.ShapeDtypeStruct((n_blk, half, width), BF),
            scratch_shapes=chunks + [whole_panel] + values,
            cost_estimate=cost(9),
            name="spread_own" if own else "spread_rest",
        )(places, row_list, cols, panel_back)

    rest = spread(False)
    rest = swapped(rest, "blk", n_blk, 1)
    terms = spread(True)
    terms, rest, arrived = lax.optimization_barrier((terms, rest, arrived))
    terms = (terms.astype(F32) + rest.astype(F32)).astype(BF)
    received = exchange(terms, ("blk", "rep"), planes)
    mine = jnp.sum(arrived, axis=0)
    grad_bias = mine[share * spans : share * spans + spans].reshape(hidden)
    shares = mine[: share * spans]
    for bits in (4, 1):
        shares = jnp.stack(
            [shares] + [swapped(shares, "rep", n_rep, bits * d) for d in range(1, 4)]
        )
    low, high = jnp.bitwise_and(place, 3), jnp.right_shift(place, 2)
    for axis, code in ((0, low), (1, high)):
        parts_of = lambda order: jnp.stack([lax.index_in_dim(shares, i, axis, False) for i in order], axis)
        shares = jnp.where(jnp.bitwise_and(code, 1) == 1, parts_of((1, 0, 3, 2)), shares)
        shares = jnp.where(jnp.bitwise_and(code, 2) == 2, parts_of((2, 3, 0, 1)), shares)
    shares = shares.swapaxes(0, 1).reshape(n_rep, spans, share, LANES)
    grad_weight = shares.swapaxes(1, 2).reshape(width, hidden)

    grad_features = pl.pallas_call(
        close_kernel,
        in_specs=[VMEM, VMEM],
        out_specs=VMEM,
        out_shape=jax.ShapeDtypeStruct((piece_rows, width), BF),
        cost_estimate=cost(1),
        name="close",
    )(received, back)
    return (activations, grad_features, grad_weight, grad_bias)


def solution(mesh):
    return jax.shard_map(
        layer,
        mesh=mesh,
        in_specs=(
            P(("blk", "rep"), None),
            P("blk", None, "rep", None),
            P("blk", None, "rep", None),
            P(),
            P(),
            P("blk", None),
            P("blk"),
        ),
        out_specs=(P(("blk", "rep"), None), P(("blk", "rep"), None), P(), P()),
        check_vma=False,
    )
```

time: 170 us -> 166 us (0.976)
  waiting for transfers between devices: 60.3 us -> 8.06 us
  blocking collectives: 38.5 us -> 68.2 us
  Pallas kernels: 27.6 us -> 49.1 us
  starting transfers between devices: 31.9 us -> 27.2 us
  other arithmetic: 0.1 us -> 4.4 us
  local copies, waits for them, and re-layouts: 8.87 us -> 5.92 us
    all_to_all x4 -> x2, waiting for transfers between devices: 38.8 us -> 8.04 us  [exchange(): lax.all_to_all(parts, axis, split_axis=0, concat_axis=0, tiled=True, axis...]
    all_to_all x1 -> x3, blocking collectives: 38.5 us -> 68.2 us  [exchange(): lax.all_to_all(parts, axis, split_axis=0, concat_axis=0, tiled=True, axis...]
    ppermute x4 -> x9, waiting for transfers between devices: 21.5 us -> 0.02 us  [swapped(): return lax.ppermute(value, axis, [(i, i ^ bits) for i in range(count)])]
    all_to_all x4 -> x2, starting transfers between devices: 30.1 us -> 8.79 us  [exchange(): lax.all_to_all(parts, axis, split_axis=0, concat_axis=0, tiled=True, axis...]
    pallas_call x2 -> x4, Pallas kernels: 20.5 us -> 41.7 us  [the longest x2 19.9 us: spread(): pl.pallas_call(functools.partial(spread_kernel, own), in_specs=[SMEM, ANY...]
    ppermute x4 -> x9, starting transfers between devices: 1.79 us -> 18.4 us  [swapped(): return lax.ppermute(value, axis, [(i, i ^ bits) for i in range(count)])]
    convert_element_type x0 -> x1, other arithmetic: none -> 1.97 us  [layer(): terms = (terms.astype(F32) + rest.astype(F32)).astype(BF)]
    broadcast_in_dim x3 -> x2, local copies, waits for them, and re-layouts: 2.77 us -> 0.81 us  [the longest x1 0.71 us: layer(): arrived = exchange(jnp.broadcast_to(mine, (n_blk, *mine.shape)), 'blk')]
  transfers between devices with their start and end apart: 8 -> 11, of which waited for: 5 -> 1; matrix products, arithmetic and copies ran while one was open for 2% -> 5% of each run, Pallas kernels for 7% -> 14%
where the time goes in v3:
time: 166 us; the launch traced here: 164 us
  blocking collectives  68.2 us (41%)
  Pallas kernels  49.1 us (30%)
  starting transfers between devices  27.2 us (16%)
  waiting for transfers between devices  8.06 us (5%)
  local copies, waits for them, and re-layouts  5.92 us (4%)
  other arithmetic  4.4 us (3%)
    all_to_all x3, blocking collectives, exchange(): lax.all_to_all(parts, axis, split_axis=0, concat_axis=0, tiled=True, axis...  68.2 us
    pallas_call x2, Pallas kernels, spread(): pl.pallas_call(functools.partial(spread_kernel, own), in_specs=[SMEM, ANY...  19.9 us
    ppermute x9, starting transfers between devices, swapped(): return lax.ppermute(value, axis, [(i, i ^ bits) for i in range(count)])  18.4 us
    pallas_call x1, Pallas kernels, layer(): pl.pallas_call(functools.partial(gather_sum_kernel, True), in_specs=[SMEM...  11.3 us
    pallas_call x1, Pallas kernels, layer(): pl.pallas_call(functools.partial(gather_sum_kernel, False), in_specs=[SME...  10.6 us
    all_to_all x2, starting transfers between devices, exchange(): lax.all_to_all(parts, axis, split_axis=0, concat_axis=0, tiled=True, axis...  8.79 us
    all_to_all x2, waiting for transfers between devices, exchange(): lax.all_to_all(parts, axis, split_axis=0, concat_axis=0, tiled=True, axis...  8.04 us
    pallas_call x1, Pallas kernels, layer(): pl.pallas_call(dense_kernel, grid_spec=pltpu.PrefetchScalarGridSpec(num_s...  3.41 us
  transfers between devices with their start and end apart: 11, of which 1 were waited for; matrix products, arithmetic and copies ran while one was open for 5% of the time, Pallas kernels for 14%

profile of v3, /device:TPU:1, one launch (start us, length us, event | category | flops | bytes accessed | tf_op | source)
XLA Modules:
  0.0 163.7 jit_solution(8614468697986324587)
XLA Ops:
  0.6 0.0 copy-start.3
  0.7 0.9 fusion.4
  1.6 0.1 maximum_bitcast_fusion
  1.7 0.1 broadcast_in_dim.6
  1.8 16.5 %all_to_all.25.table_ref = bf16[16,128,128]{2,1,0:T(8,128)(2,1)S(1)} all-to-all(bf16[16,128,128]{2,1,0:T(8,128)(2,1)S(1)} %bitcast.45), channel_id=1, replica_groups={{0,1,32,33,64,65,96,97,128,129,160,161,192,193,224,225},{2,3,34,35,66,6..., dimensions={0} | all-to-all | bytes 1048576 | tf_op jit(solution)/shard_map/all_to_all | solution.py:31
  18.3 2.7 %collective-permute-start.1 = (bf16[16,128,128]{2,1,0:T(8,128)(2,1)S(1)}, bf16[16,128,128]{2,1,0:T(8,128)(2,1)S(1)}, u32[]{:S(2)}, u32[]{:S(2)}) collective-permute-start(bf16[16,128,128]{2,1,0:T(8,128)(2,1)S(1)} %all_to_all.25.table_ref), channel_id=1, source_target_pairs={{0,16},{16,0},{32,48},{48,32},{64,80},{80,64},{96,112},{112,96},{1... | collective-permute-start | bytes 1572872 | tf_op jit(solution)/shard_map/ppermute | solution.py:37
  21.0 1.6 collective-permute-start
  22.6 0.6 pad_add_fusion.1.place_ref
  23.2 0.6 reshape.45.rows_ref
  23.8 2.2 %count.1.refs_0_ = f32[32,128]{1,0:T(8,128)} custom-call(s32[32,256]{1,0:T(8,128)} %reshape.45.rows_ref), custom_call_target="tpu_custom_call" | custom-call | bytes 6000000 | tf_op jit(solution)/shard_map/count/pallas_call | solution.py:283
  26.0 0.0 collective-permute-done
  26.1 0.7 copy.18
  26.7 0.7 shift_right_arithmetic.16.cols_ref
  27.4 10.6 %gather_own.1.refs_1_ = f32[4096,128]{1,0:T(8,128)} custom-call(s32[2]{0:T(128)} %pad_add_fusion.1.place_ref, s32[16384]{0:T(1024)} %bitcast.46, s32[64,256]{1,0:T(8,128)} %shift_right_arithmetic.16.cols_ref, bf16[16,128,128]{2,1,0:T(8,128)(2,1)} %copy-done.1), custom_call_target="tpu_custom_call" | custom-call | bytes 30000000 | tf_op jit(solution)/shard_map/gather_own/pallas_call | solution.py:296
  38.0 0.0 collective-permute-done.1.table_ref
  38.0 0.0 copy-start.2
  38.0 0.8 copy-done.2
  38.8 11.3 %gather_rest.1 = bf16[16,136,128]{2,1,0:T(8,128)(2,1)} custom-call(s32[2]{0:T(128)} %pad_add_fusion.1.place_ref, s32[16384]{0:T(1024)} %bitcast.47, s32[64,256]{1,0:T(8,128)} %shift_right_arithmetic.16.cols_ref, bf16[16,128,128]{2,1,0:T(8,128)(2,1)} %copy-done.2, f32[32,128]{1,0:T(8,128)} %count.1.refs_0_, f32[4096,128]{1,0:T(8,128)} %gather_own.1.refs_1_), custom_call_target="tpu_custom_call" | custom-call | bytes 30000000 | tf_op jit(solution)/shard_map/gather_rest/pallas_call | solution.py:305
  50.1 28.8 %all_to_all.26.parts_ref = bf16[16,136,128]{2,1,0:T(8,128)(2,1)} all-to-all(bf16[16,136,128]{2,1,0:T(8,128)(2,1)} %gather_rest.1), channel_id=1, replica_groups=mesh['blk'=16,'rep'=16] {'rep'}, dimensions={0} | all-to-all | bytes 1114112 | tf_op jit(solution)/shard_map/all_to_all | solution.py:31
  78.8 3.4 %dense.1 = (bf16[256,256]{1,0:T(8,128)(2,1)}, bf16[256,128]{1,0:T(8,128)(2,1)}, bf16[16,152,128]{2,1,0:T(8,128)(2,1)}) custom-call(s32[2]{0:T(128)} %pad_add_fusion.1.place_ref, bf16[16,136,128]{2,1,0:T(8,128)(2,1)} %all_to_all.26.parts_ref, bf16[256,128]{1,0:T(8,128)(2,1)} %feats_ref.1, bf16[4096,256]{1,0:T(8,128)(2,1)} %upstream_ref.1, ...), custom_call_target="tpu_custom_call" | custom-call | bytes 9000000 | tf_op jit(solution)/shard_map/dense/pallas_call | solution.py:322
  82.2 22.9 %all_to_all.27.table_ref = bf16[16,152,128]{2,1,0:T(8,128)(2,1)} all-to-all(bf16[16,152,128]{2,1,0:T(8,128)(2,1)} %get-tuple-element.11), channel_id=1, replica_groups=mesh['blk'=16,'rep'=16] {'rep'}, dimensions={0} | all-to-all | bytes 1245184 | tf_op jit(solution)/shard_map/all_to_all | solution.py:31
  105.2 9.9 %spread_rest.1 = bf16[16,128,128]{2,1,0:T(8,128)(2,1)} custom-call(s32[2]{0:T(128)} %pad_add_fusion.1.place_ref, s32[16384]{0:T(1024)} %bitcast.48, s32[64,256]{1,0:T(8,128)} %shift_right_arithmetic.16.cols_ref, bf16[16,152,128]{2,1,0:T(8,128)(2,1)} %all_to_all.27.table_ref), custom_call_target="tpu_custom_call" | custom-call | bytes 27000000 | tf_op jit(solution)/shard_map/spread_rest/pallas_call | solution.py:364
  115.1 4.2 %collective-permute-start.2 = (bf16[16,128,128]{2,1,0:T(8,128)(2,1)}, bf16[16,128,128]{2,1,0:T(8,128)(2,1)S(1)}, u32[]{:S(2)}, u32[]{:S(2)}) collective-permute-start(bf16[16,128,128]{2,1,0:T(8,128)(2,1)} %spread_rest.1), channel_id=1, source_target_pairs={{0,16},{16,0},{32,48},{48,32},{64,80},{80,64},{96,112},{112,96},{1... | collective-permute-start | bytes 1572872 | tf_op jit(solution)/shard_map/ppermute | solution.py:37
  119.3 0.9 convert_reduce_fusion
  120.2 0.7 broadcast_in_dim.7
  120.9 3.7 %all-to-all-start.3 = ((f32[16,24,128]{2,1,0:T(8,128)}), f32[16,24,128]{2,1,0:T(8,128)S(1)}, u32[]{:S(2)}, u32[]{:S(2)}) async-start(f32[16,24,128]{2,1,0:T(8,128)} %broadcast_in_dim.7), calls=%async_computation.3 | async-start | bytes 393216 | tf_op jit(solution)/shard_map/all_to_all | solution.py:31
  124.6 9.9 %spread_own.1 = bf16[16,128,128]{2,1,0:T(8,128)(2,1)} custom-call(s32[2]{0:T(128)} %pad_add_fusion.1.place_ref, s32[16384]{0:T(1024)} %bitcast.49, s32[64,256]{1,0:T(8,128)} %shift_right_arithmetic.16.cols_ref, bf16[16,152,128]{2,1,0:T(8,128)(2,1)} %all_to_all.27.table_ref), custom_call_target="tpu_custom_call" | custom-call | bytes 27000000 | tf_op jit(solution)/shard_map/spread_own/pallas_call | solution.py:364
  134.5 0.0 all-to-all-done.3
  134.5 0.0 collective-permute-done.2
  134.5 0.3 collective-permute-start.3
  134.9 2.1 %collective-permute-start.4 = (f32[16,128]{1,0:T(8,128)S(1)}, f32[16,128]{1,0:T(8,128)S(1)}, u32[]{:S(2)}, u32[]{:S(2)}) collective-permute-start(f32[16,128]{1,0:T(8,128)S(1)} %get-tuple-element.35), channel_id=1, source_target_pairs={{0,8},{1,9},{2,10},{3,11},{4,12},{5,13},{6,14},{7,15},{8,0},{9,1},... | collective-permute-start | bytes 24584 | tf_op jit(solution)/shard_map/ppermute | solution.py:37
  137.0 3.3 %collective-permute-start.5 = (f32[16,128]{1,0:T(8,128)S(1)}, f32[16,128]{1,0:T(8,128)S(1)}, u32[]{:S(2)}, u32[]{:S(2)}) collective-permute-start(f32[16,128]{1,0:T(8,128)S(1)} %get-tuple-element.35), channel_id=1, source_target_pairs={{0,12},{1,13},{2,14},{3,15},{4,8},{5,9},{6,10},{7,11},{8,4},{9,5},... | collective-permute-start | bytes 24584 | tf_op jit(solution)/shard_map/ppermute | solution.py:37
  140.3 2.0 %add_convert_fusion = bf16[16,128,128]{2,1,0:T(8,128)(2,1)} fusion(bf16[16,128,128]{2,1,0:T(8,128)(2,1)S(1)} %collective-permute-done.2, bf16[16,128,128]{2,1,0:T(8,128)(2,1)} %spread_own.1), kind=kLoop, calls=%fused_computation | loop fusion | flops 1048576 | bytes 1572864 | tf_op jit(solution)/shard_map/convert_element_type | solution.py:378
  142.3 0.0 collective-permute-done.3
  142.3 0.0 collective-permute-done.4
  142.3 0.0 collective-permute-done.5
  142.3 0.4 collective-permute-start.6
  142.7 2.9 %collective-permute-start.7 = (f32[4,16,128]{2,1,0:T(8,128)S(1)}, f32[4,16,128]{2,1,0:T(8,128)S(1)}, u32[]{:S(2)}, u32[]{:S(2)}) collective-permute-start(f32[4,16,128]{2,1,0:T(8,128)S(1)} %get-tuple-element.33), channel_id=1, source_target_pairs={{0,3},{1,2},{2,1},{3,0},{4,7},{5,6},{6,5},{7,4},{8,11},{9,10},{10,... | collective-permute-start | bytes 98312 | tf_op jit(solution)/shard_map/ppermute | solution.py:37
  145.5 1.0 collective-permute-start.8
  146.5 0.6 slice_bitcast_fusion
  147.1 5.1 %all-to-all-start.4 = ((bf16[16,128,128]{2,1,0:T(8,128)(2,1)}), bf16[16,128,128]{2,1,0:T(8,128)(2,1)S(1)}, u32[]{:S(2)}, u32[]{:S(2)}) async-start(bf16[16,128,128]{2,1,0:T(8,128)(2,1)} %add_convert_fusion), calls=%async_computation.4 | async-start | bytes 1048576 | tf_op jit(solution)/shard_map/all_to_all | solution.py:31
  152.2 0.0 collective-permute-done.6
  152.2 0.0 collective-permute-done.7
  152.3 0.0 collective-permute-done.8
  152.4 0.7 maximum_select_fusion.3
  153.1 8.0 %all-to-all-done.4.terms_ref = bf16[16,128,128]{2,1,0:T(8,128)(2,1)S(1)} async-done(((bf16[16,128,128]{2,1,0:T(8,128)(2,1)}), bf16[16,128,128]{2,1,0:T(8,128)(2,1)S(1)}, u32[]{:S(2)}, u32[]{:S(2)}) %all-to-all-start.4) | async-done | bytes 524320 | tf_op jit(solution)/shard_map/all_to_all | solution.py:31
  161.1 0.8 copy-done
  161.9 1.8 %close.1 = bf16[256,128]{1,0:T(8,128)(2,1)} custom-call(bf16[16,128,128]{2,1,0:T(8,128)(2,1)} %copy-done, bf16[256,128]{1,0:T(8,128)(2,1)} %get-tuple-element.14.back_ref), custom_call_target="tpu_custom_call" | custom-call | bytes 3000000 | tf_op jit(solution)/shard_map/close/pallas_call | solution.py:395
  (19 shorter events, 0.2 us)
Async XLA Ops:
  0.6 20.4 %copy-start.3 = (s32[1,16,2,256]{3,2,1,0:T(2,128)S(1)}, s32[1,16,2,256]{3,2,1,0:T(2,128)}, u32[]{:S(2)}) copy-start(s32[1,16,2,256]{3,2,1,0:T(2,128)} %param.8) | copy-start | bytes 98308
  0.6 20.4 %copy-start.4 = (s32[1,16,2,256]{3,2,1,0:T(2,128)S(1)}, s32[1,16,2,256]{3,2,1,0:T(2,128)}, u32[]{:S(2)}) copy-start(s32[1,16,2,256]{3,2,1,0:T(2,128)} %param.9) | copy-start | bytes 98308
  18.3 9.1 %copy-start.1 = (bf16[16,128,128]{2,1,0:T(8,128)(2,1)}, bf16[16,128,128]{2,1,0:T(8,128)(2,1)S(1)}, u32[]{:S(2)}) copy-start(bf16[16,128,128]{2,1,0:T(8,128)(2,1)S(1)} %all_to_all.25.table_ref) | copy-start | bytes 1572868
  18.3 19.7 %collective-permute-start.1 = (bf16[16,128,128]{2,1,0:T(8,128)(2,1)S(1)}, bf16[16,128,128]{2,1,0:T(8,128)(2,1)S(1)}, u32[]{:S(2)}, u32[]{:S(2)}) collective-permute-start(bf16[16,128,128]{2,1,0:T(8,128)(2,1)S(1)} %all_to_all.25.table_ref), channel_id=1, source_target_pairs={{0,16},{16,0},{32,48},{48,32},{64,80},{80,64},{96,112},{112,96},{1... | collective-permute-start | bytes 1572872 | tf_op jit(solution)/shard_map/ppermute | solution.py:37
  21.0 5.0 %collective-permute-start = (s32[16,2,256]{2,1,0:T(2,128)S(1)}, s32[16,2,256]{2,1,0:T(2,128)S(1)}, u32[]{:S(2)}, u32[]{:S(2)}) collective-permute-start(s32[16,2,256]{2,1,0:T(2,128)S(1)} %or_bitcast_fusion), channel_id=1, source_target_pairs={{0,1},{1,0},{2,3},{3,2},{4,5},{5,4},{6,7},{7,6},{8,9},{9,8},{10,11... | collective-permute-start | bytes 98312 | tf_op jit(solution)/shard_map/ppermute | solution.py:37
  38.0 0.8 copy-start.2
  115.1 19.4 %collective-permute-start.2 = (bf16[16,128,128]{2,1,0:T(8,128)(2,1)}, bf16[16,128,128]{2,1,0:T(8,128)(2,1)S(1)}, u32[]{:S(2)}, u32[]{:S(2)}) collective-permute-start(bf16[16,128,128]{2,1,0:T(8,128)(2,1)} %spread_rest.1), channel_id=1, source_target_pairs={{0,16},{16,0},{32,48},{48,32},{64,80},{80,64},{96,112},{112,96},{1... | collective-permute-start | bytes 1572872 | tf_op jit(solution)/shard_map/ppermute | solution.py:37
  120.9 13.6 %all-to-all-start.3 = ((f32[16,24,128]{2,1,0:T(8,128)}), f32[16,24,128]{2,1,0:T(8,128)S(1)}, u32[]{:S(2)}, u32[]{:S(2)}) async-start(f32[16,24,128]{2,1,0:T(8,128)} %broadcast_in_dim.7), calls=%async_computation.3 | async-start | bytes 393216 | tf_op jit(solution)/shard_map/all_to_all | solution.py:31
  134.5 7.7 %collective-permute-start.3 = (f32[16,128]{1,0:T(8,128)S(1)}, f32[16,128]{1,0:T(8,128)S(1)}, u32[]{:S(2)}, u32[]{:S(2)}) collective-permute-start(f32[16,128]{1,0:T(8,128)S(1)} %get-tuple-element.35), channel_id=1, source_target_pairs={{0,4},{1,5},{2,6},{3,7},{4,0},{5,1},{6,2},{7,3},{8,12},{9,13},{10,... | collective-permute-start | bytes 24584 | tf_op jit(solution)/shard_map/ppermute | solution.py:37
  134.9 7.4 %collective-permute-start.4 = (f32[16,128]{1,0:T(8,128)S(1)}, f32[16,128]{1,0:T(8,128)S(1)}, u32[]{:S(2)}, u32[]{:S(2)}) collective-permute-start(f32[16,128]{1,0:T(8,128)S(1)} %get-tuple-element.35), channel_id=1, source_target_pairs={{0,8},{1,9},{2,10},{3,11},{4,12},{5,13},{6,14},{7,15},{8,0},{9,1},... | collective-permute-start | bytes 24584 | tf_op jit(solution)/shard_map/ppermute | solution.py:37
  137.0 5.3 %collective-permute-start.5 = (f32[16,128]{1,0:T(8,128)S(1)}, f32[16,128]{1,0:T(8,128)S(1)}, u32[]{:S(2)}, u32[]{:S(2)}) collective-permute-start(f32[16,128]{1,0:T(8,128)S(1)} %get-tuple-element.35), channel_id=1, source_target_pairs={{0,12},{1,13},{2,14},{3,15},{4,8},{5,9},{6,10},{7,11},{8,4},{9,5},... | collective-permute-start | bytes 24584 | tf_op jit(solution)/shard_map/ppermute | solution.py:37
  142.3 9.9 %collective-permute-start.6 = (f32[4,16,128]{2,1,0:T(8,128)S(1)}, f32[4,16,128]{2,1,0:T(8,128)S(1)}, u32[]{:S(2)}, u32[]{:S(2)}) collective-permute-start(f32[4,16,128]{2,1,0:T(8,128)S(1)} %get-tuple-element.33), channel_id=1, source_target_pairs={{0,1},{1,0},{2,3},{3,2},{4,5},{5,4},{6,7},{7,6},{8,9},{9,8},{10,11... | collective-permute-start | bytes 98312 | tf_op jit(solution)/shard_map/ppermute | solution.py:37
  142.7 9.6 %collective-permute-start.7 = (f32[4,16,128]{2,1,0:T(8,128)S(1)}, f32[4,16,128]{2,1,0:T(8,128)S(1)}, u32[]{:S(2)}, u32[]{:S(2)}) collective-permute-start(f32[4,16,128]{2,1,0:T(8,128)S(1)} %get-tuple-element.33), channel_id=1, source_target_pairs={{0,3},{1,2},{2,1},{3,0},{4,7},{5,6},{6,5},{7,4},{8,11},{9,10},{10,... | collective-permute-start | bytes 98312 | tf_op jit(solution)/shard_map/ppermute | solution.py:37
  145.5 6.7 %collective-permute-start.8 = (f32[4,16,128]{2,1,0:T(8,128)S(1)}, f32[4,16,128]{2,1,0:T(8,128)S(1)}, u32[]{:S(2)}, u32[]{:S(2)}) collective-permute-start(f32[4,16,128]{2,1,0:T(8,128)S(1)} %get-tuple-element.33), channel_id=1, source_target_pairs={{0,2},{1,3},{2,0},{3,1},{4,6},{5,7},{6,4},{7,5},{8,10},{9,11},{10,... | collective-permute-start | bytes 98312 | tf_op jit(solution)/shard_map/ppermute | solution.py:37
  147.1 14.0 %all-to-all-start.4 = ((bf16[16,128,128]{2,1,0:T(8,128)(2,1)}), bf16[16,128,128]{2,1,0:T(8,128)(2,1)S(1)}, u32[]{:S(2)}, u32[]{:S(2)}) async-start(bf16[16,128,128]{2,1,0:T(8,128)(2,1)} %add_convert_fusion), calls=%async_computation.4 | async-start | bytes 1048576 | tf_op jit(solution)/shard_map/all_to_all | solution.py:31
  161.1 0.8 copy-start

commit v4 on v3

--- a/solution.py
+++ b/solution.py
@@ -205,7 +205,7 @@
 
 def dense_kernel(
     place_ref, parts_ref, feats_ref, upstream_ref, mask_ref, weight_ref, bias_ref,
-    act_ref, back_ref, sends_ref,
+    act_ref, back_ref, sends_ref, wsends_ref, wpart_ref,
 ):
     piece_rows, width = feats_ref.shape
     half = piece_rows // 2
@@ -229,22 +229,44 @@
     back = back.astype(BF)
     back_ref[...] = back
     sides = [side.astype(BF) for side in packed(back.astype(F32))]
-    weight_part = lax.dot_general(mixed, grad, TN, preferred_element_type=F32).astype(BF)
+    for p in range(sends_ref.shape[0]):
+        sends_ref[p] = sides[p % 2]
+    wpart_ref[...] = lax.dot_general(mixed, grad, TN, preferred_element_type=F32)
     bias_part = jnp.sum(grad.astype(F32), axis=0, keepdims=True)
     spans = range(0, bias_part.shape[1], LANES)
     rest = jnp.zeros((8 - len(spans), LANES), F32)
-    bias_part = jnp.concatenate([bias_part[:, c : c + LANES] for c in spans] + [rest], 0).astype(BF)
-    share = width // sends_ref.shape[0]
-    for p in range(sends_ref.shape[0]):
-        pieces = [weight_part[p * share : (p + 1) * share, c : c + LANES] for c in spans]
-        sends_ref[p] = jnp.concatenate([sides[p % 2], *pieces, bias_part], 0)
-
-
-def close_kernel(terms_ref, back_ref, out_ref):
-    sums = [terms_ref[s].astype(F32) for s in range(2)]
+    bias_part = jnp.concatenate([bias_part[:, c : c + LANES] for c in spans] + [rest], 0)
+    count = wsends_ref.shape[0]
+    share = width // count
+    for d in range(count):
+        chip = jnp.bitwise_xor(jnp.right_shift(place_ref[1], 1), d)
+        rows = wpart_ref[pl.ds(pl.multiple_of(chip * share, share), share), :]
+        wsends_ref[d] = jnp.concatenate([rows[:, c : c + LANES] for c in spans] + [bias_part], 0)
+
+
+def join_kernel(place_ref, own_ref, rest_ref, shares_ref, out_ref):
+    rows = own_ref.shape[1]
+    share = (out_ref.shape[1] - rows) // 2
+    start = pl.multiple_of(jnp.bitwise_and(place_ref[0], 1) * share, share)
+    shares = shares_ref[pl.ds(start, share), :]
+    high = shares.astype(BF)
+    both = jnp.concatenate([high, (shares - high.astype(F32)).astype(BF)], 0)
+    for p in range(out_ref.shape[0]):
+        out_ref[p, :rows, :] = (own_ref[p].astype(F32) + rest_ref[p].astype(F32)).astype(BF)
+        out_ref[p, rows:, :] = both
+
+
+def close_kernel(terms_ref, back_ref, out_ref, wgrad_ref):
+    rows = back_ref.shape[0] // 2
+    sums = [terms_ref[s, :rows].astype(F32) for s in range(2)]
     for p in range(2, terms_ref.shape[0]):
-        sums[p % 2] += terms_ref[p].astype(F32)
+        sums[p % 2] += terms_ref[p, :rows].astype(F32)
     out_ref[...] = (back_ref[...].astype(F32) + unpacked(sums[0], sums[1])).astype(BF)
+    share = (terms_ref.shape[1] - rows) // 2
+    for p in range(terms_ref.shape[0]):
+        both = terms_ref[p, rows : rows + share].astype(F32) + terms_ref[p, rows + share :].astype(F32)
+        j, c = p // 2, p % 2
+        wgrad_ref[j * share : (j + 1) * share, c * LANES : (c + 1) * LANES] = both
 
 
 def layer(features, edge_rows, edge_cols, weight, bias, upstream, train_mask):
@@ -271,6 +293,7 @@
 
     other_table = swapped(table, "blk", n_blk, 1)
 
+    places = jnp.stack([place, panel]).astype(jnp.int32)
     edges = jnp.bitwise_or(edge_rows[0], jnp.left_shift(edge_cols[0], 16))
     others = swapped(edges, "rep", n_rep, 1)
     second = jnp.bitwise_and(place, 1) == 1
@@ -286,11 +309,11 @@
         out_specs=VMEM,
         out_shape=jax.ShapeDtypeStruct((panel_rows // LANES, LANES), F32),
         cost_estimate=cost(2),
-        name="count",
+        compiler_params=pltpu.CompilerParams(vmem_limit_bytes=8 << 20),
+    name="count",
     )(own_rows)
     chunks = [pltpu.SMEM((CHUNK,), jnp.int32)] * 2 + [pltpu.SemaphoreType.DMA((2,))]
 
-    places = jnp.stack([place, panel]).astype(jnp.int32)
     whole_panel = pltpu.VMEM((panel_rows, width), F32)
     values = [pltpu.VMEM((slots, width), F32)] * 2
     partial = pl.pallas_call(
@@ -300,6 +323,7 @@
         out_shape=jax.ShapeDtypeStruct((panel_rows, width), F32),
         scratch_shapes=chunks + values + [whole_panel] * TOTALS,
         cost_estimate=cost(10),
+        compiler_params=pltpu.CompilerParams(vmem_limit_bytes=26 << 20),
         name="gather_own",
     )(places, row_list, cols, table)
     sends = pl.pallas_call(
@@ -312,14 +336,15 @@
         + [whole_panel, pltpu.SemaphoreType.DMA]
         + [whole_panel] * TOTALS,
         cost_estimate=cost(10),
+        compiler_params=pltpu.CompilerParams(vmem_limit_bytes=28 << 20),
         name="gather_rest",
     )(places, row_list, cols, other_table, counts, partial)
     parts = exchange(sends, "rep")
 
-    share = width // n_rep
+    share = width // (n_blk // 2)
     spans = hidden // LANES
-    extra = share * spans + 8
-    activations, back, sends = pl.pallas_call(
+    w_rows = share * spans + 8
+    activations, back, sends, wsends = pl.pallas_call(
         dense_kernel,
         grid_spec=pltpu.PrefetchScalarGridSpec(
             num_scalar_prefetch=1,
@@ -335,15 +360,19 @@
             out_specs=[
                 pl.BlockSpec((piece_rows, hidden), lambda i, s: (0, 0)),
                 pl.BlockSpec((piece_rows, width), lambda i, s: (0, 0)),
-                pl.BlockSpec((n_rep, half + extra, width), lambda i, s: (0, 0, 0)),
+                pl.BlockSpec((n_rep, half, width), lambda i, s: (0, 0, 0)),
+                pl.BlockSpec((n_blk // 2, w_rows, LANES), lambda i, s: (0, 0, 0)),
             ],
+            scratch_shapes=[pltpu.VMEM((width, hidden), F32)],
         ),
         out_shape=[
             jax.ShapeDtypeStruct((piece_rows, hidden), BF),
             jax.ShapeDtypeStruct((piece_rows, width), BF),
-            jax.ShapeDtypeStruct((n_rep, half + extra, width), BF),
+            jax.ShapeDtypeStruct((n_rep, half, width), BF),
+            jax.ShapeDtypeStruct((n_blk // 2, w_rows, LANES), F32),
         ],
         cost_estimate=cost(3),
+        compiler_params=pltpu.CompilerParams(vmem_limit_bytes=12 << 20),
         name="dense",
     )(
         places,
@@ -357,8 +386,13 @@
 
     panel_back = exchange(sends, "rep")
 
-    mine = jnp.sum(panel_back[:, half:].astype(F32), axis=0)
-    arrived = exchange(jnp.broadcast_to(mine, (n_blk, *mine.shape)), "blk")
+    mine = wsends.reshape(-1, 2, w_rows, LANES)
+    near, far = mine[:, 0], mine[:, 1]
+    others = [swapped(v, "blk", n_blk, d) for v, d in ((near, 1), (far, 2), (far, 3))]
+    near = near + others[0] + others[1] + others[2]
+    others = [swapped(near[d], "blk", n_blk, 4 * d) for d in range(1, 4)]
+    mine = near[0] + others[0] + others[1] + others[2]
+    others = [swapped(mine, "rep", n_rep, d) for d in (4, 8, 12)]
 
     def spread(own):
         return pl.pallas_call(
@@ -368,36 +402,37 @@
             out_shape=jax.ShapeDtypeStruct((n_blk, half, width), BF),
             scratch_shapes=chunks + [whole_panel] + values,
             cost_estimate=cost(9),
+            compiler_params=pltpu.CompilerParams(vmem_limit_bytes=10 << 20),
             name="spread_own" if own else "spread_rest",
         )(places, row_list, cols, panel_back)
 
     rest = spread(False)
-    rest = swapped(rest, "blk", n_blk, 1)
+    arrived = swapped(rest, "blk", n_blk, 1)
+    mine = mine + others[0] + others[1] + others[2]
+    others = [swapped(mine, "rep", n_rep, d) for d in (1, 2, 3)]
     terms = spread(True)
-    terms, rest, arrived = lax.optimization_barrier((terms, rest, arrived))
-    terms = (terms.astype(F32) + rest.astype(F32)).astype(BF)
-    received = exchange(terms, ("blk", "rep"), planes)
-    mine = jnp.sum(arrived, axis=0)
+    mine = mine + others[0] + others[1] + others[2]
     grad_bias = mine[share * spans : share * spans + spans].reshape(hidden)
-    shares = mine[: share * spans]
-    for bits in (4, 1):
-        shares = jnp.stack(
-            [shares] + [swapped(shares, "rep", n_rep, bits * d) for d in range(1, 4)]
-        )
-    low, high = jnp.bitwise_and(place, 3), jnp.right_shift(place, 2)
-    for axis, code in ((0, low), (1, high)):
-        parts_of = lambda order: jnp.stack([lax.index_in_dim(shares, i, axis, False) for i in order], axis)
-        shares = jnp.where(jnp.bitwise_and(code, 1) == 1, parts_of((1, 0, 3, 2)), shares)
-        shares = jnp.where(jnp.bitwise_and(code, 2) == 2, parts_of((2, 3, 0, 1)), shares)
-    shares = shares.swapaxes(0, 1).reshape(n_rep, spans, share, LANES)
-    grad_weight = shares.swapaxes(1, 2).reshape(width, hidden)
-
-    grad_features = pl.pallas_call(
+    joined = pl.pallas_call(
+        join_kernel,
+        in_specs=[SMEM, VMEM, VMEM, VMEM],
+        out_specs=VMEM,
+        out_shape=jax.ShapeDtypeStruct((n_blk, half + 2 * share, width), BF),
+        cost_estimate=cost(1),
+        compiler_params=pltpu.CompilerParams(vmem_limit_bytes=8 << 20),
+        name="join",
+    )(places, terms, arrived, mine)
+    received = exchange(joined, ("blk", "rep"), planes)
+    grad_features, grad_weight = pl.pallas_call(
         close_kernel,
         in_specs=[VMEM, VMEM],
-        out_specs=VMEM,
-        out_shape=jax.ShapeDtypeStruct((piece_rows, width), BF),
+        out_specs=[VMEM, VMEM],
+        out_shape=[
+            jax.ShapeDtypeStruct((piece_rows, width), BF),
+            jax.ShapeDtypeStruct((width, hidden), F32),
+        ],
         cost_estimate=cost(1),
+        compiler_params=pltpu.CompilerParams(vmem_limit_bytes=8 << 20),
         name="close",
     )(received, back)
     return (activations, grad_features, grad_weight, grad_bias)

time: 166 us -> 149 us (0.90)
  blocking collectives: 68.2 us -> 44.7 us
  waiting for transfers between devices: 8.06 us -> 23.4 us
  Pallas kernels: 49.1 us -> 41.6 us
  starting transfers between devices: 27.2 us -> 33.7 us
  local copies, waits for them, and re-layouts: 5.92 us -> 1.75 us
  other arithmetic: 4.4 us -> 0.31 us
    all_to_all x3 -> x2, blocking collectives: 68.2 us -> 44.7 us  [exchange(): lax.all_to_all(parts, axis, split_axis=0, concat_axis=0, tiled=True, axis...]
    ppermute x9 -> x15, waiting for transfers between devices: 0.02 us -> 12.2 us  [swapped(): return lax.ppermute(value, axis, [(i, i ^ bits) for i in range(count)])]
    ppermute x9 -> x15, starting transfers between devices: 18.4 us -> 26.6 us  [swapped(): return lax.ppermute(value, axis, [(i, i ^ bits) for i in range(count)])]
    all_to_all x2, waiting for transfers between devices: 8.04 us -> 11.2 us  [exchange(): lax.all_to_all(parts, axis, split_axis=0, concat_axis=0, tiled=True, axis...]
    pallas_call x2, Pallas kernels: 19.9 us -> 17.1 us  [spread(): pl.pallas_call(functools.partial(spread_kernel, own), in_specs=[SMEM, ANY...]
    unnamed x11 -> x15, local copies, waits for them, and re-layouts: 2.27 us -> 0.08 us
    convert_element_type x1 -> x0, other arithmetic: 1.97 us -> none  [layer(): terms = (terms.astype(F32) + rest.astype(F32)).astype(BF)]
    pallas_call x1, Pallas kernels: 10.6 us -> 8.75 us  [layer(): pl.pallas_call(functools.partial(gather_sum_kernel, False), in_specs=[SME...]
  transfers between devices with their start and end apart: 11 -> 17, of which waited for: 1 -> 9; matrix products, arithmetic and copies ran while one was open for 5% -> 1% of each run, Pallas kernels for 14% -> 18%
where the time goes in v4:
time: 149 us; the launch traced here: 146 us
  blocking collectives  44.7 us (30%)
  Pallas kernels  41.6 us (28%)
  starting transfers between devices  33.7 us (23%)
  waiting for transfers between devices  23.4 us (16%)
  local copies, waits for them, and re-layouts  1.75 us (1%)
    all_to_all x2, blocking collectives, exchange(): lax.all_to_all(parts, axis, split_axis=0, concat_axis=0, tiled=True, axis...  44.7 us
    ppermute x15, starting transfers between devices, swapped(): return lax.ppermute(value, axis, [(i, i ^ bits) for i in range(count)])  26.6 us
    pallas_call x2, Pallas kernels, spread(): pl.pallas_call(functools.partial(spread_kernel, own), in_specs=[SMEM, ANY...  17.1 us
    ppermute x15, waiting for transfers between devices, swapped(): return lax.ppermute(value, axis, [(i, i ^ bits) for i in range(count)])  12.2 us
    all_to_all x2, waiting for transfers between devices, exchange(): lax.all_to_all(parts, axis, split_axis=0, concat_axis=0, tiled=True, axis...  11.2 us
    pallas_call x1, Pallas kernels, layer(): pl.pallas_call(functools.partial(gather_sum_kernel, True), in_specs=[SMEM...  10.5 us
    pallas_call x1, Pallas kernels, layer(): pl.pallas_call(functools.partial(gather_sum_kernel, False), in_specs=[SME...  8.75 us
    all_to_all x2, starting transfers between devices, exchange(): lax.all_to_all(parts, axis, split_axis=0, concat_axis=0, tiled=True, axis...  7.16 us
  transfers between devices with their start and end apart: 17, of which 9 were waited for; matrix products, arithmetic and copies ran while one was open for 1% of the time, Pallas kernels for 18%

profile of v4, /device:TPU:1, one launch (start us, length us, event | category | flops | bytes accessed | tf_op | source)
XLA Modules:
  0.0 146.3 jit_solution(18289048960359910014)
XLA Ops:
  0.7 0.9 fusion.3
  1.6 0.1 maximum_bitcast_fusion
  1.7 0.1 broadcast_in_dim.3
  1.8 16.5 %all_to_all.20.table_ref = bf16[16,128,128]{2,1,0:T(8,128)(2,1)S(1)} all-to-all(bf16[16,128,128]{2,1,0:T(8,128)(2,1)S(1)} %bitcast.57), channel_id=1, replica_groups={{0,1,32,33,64,65,96,97,128,129,160,161,192,193,224,225},{2,3,34,35,66,6..., dimensions={0} | all-to-all | bytes 1048576 | tf_op jit(solution)/shard_map/all_to_all | solution.py:31
  18.3 2.7 %collective-permute-start.1 = (bf16[16,128,128]{2,1,0:T(8,128)(2,1)S(1)}, bf16[16,128,128]{2,1,0:T(8,128)(2,1)S(1)}, u32[]{:S(2)}, u32[]{:S(2)}) collective-permute-start(bf16[16,128,128]{2,1,0:T(8,128)(2,1)S(1)} %all_to_all.20.table_ref), channel_id=1, source_target_pairs={{0,16},{16,0},{32,48},{48,32},{64,80},{80,64},{96,112},{112,96},{1... | collective-permute-start | bytes 1572872 | tf_op jit(solution)/shard_map/ppermute | solution.py:37
  21.0 1.6 %collective-permute-start = (s32[16,2,256]{2,1,0:T(2,128)S(1)}, s32[16,2,256]{2,1,0:T(2,128)S(1)}, u32[]{:S(2)}, u32[]{:S(2)}) collective-permute-start(s32[16,2,256]{2,1,0:T(2,128)S(1)} %or_bitcast_fusion), channel_id=1, source_target_pairs={{0,1},{1,0},{2,3},{3,2},{4,5},{5,4},{6,7},{7,6},{8,9},{9,8},{10,11... | collective-permute-start | bytes 98312 | tf_op jit(solution)/shard_map/ppermute | solution.py:37
  22.6 0.1 pad_add_fusion.1.place_ref
  22.7 0.8 count.1.refs_0_
  23.5 1.8 %collective-permute-done = s32[16,2,256]{2,1,0:T(2,128)S(1)} collective-permute-done((s32[16,2,256]{2,1,0:T(2,128)S(1)}, s32[16,2,256]{2,1,0:T(2,128)S(1)}, u32[]{:S(2)}, u32[]{:S(2)}) %collective-permute-start) | collective-permute-done | bytes 32800 | tf_op jit(solution)/shard_map/ppermute | solution.py:37
  25.5 8.7 %gather_own.1.refs_1_ = f32[4096,128]{1,0:T(8,128)S(1)} custom-call(s32[2]{0:T(128)S(1)} %pad_add_fusion.1.place_ref, s32[16384]{0:T(1024)S(1)} %bitcast.49, s32[64,256]{1,0:T(8,128)S(1)} %shift_right_arithmetic.13.cols_ref, bf16[16,128,128]{2,1,0:T(8,128)(2,1)S(1)} %all_to_all.20.table_ref), custom_call_target="tpu_custom_call" | custom-call | bytes 30000000 | tf_op jit(solution)/shard_map/gather_own/pallas_call | solution.py:319
  34.3 0.0 copy-start
  34.3 0.0 copy-start.1
  34.3 0.0 copy-start.2
  34.3 0.0 copy-start.3
  34.3 0.0 copy-start.4
  34.4 10.5 %gather_rest.1 = bf16[16,136,128]{2,1,0:T(8,128)(2,1)S(1)} custom-call(s32[2]{0:T(128)S(1)} %pad_add_fusion.1.place_ref, s32[16384]{0:T(1024)S(1)} %bitcast.50, s32[64,256]{1,0:T(8,128)S(1)} %shift_right_arithmetic.13.cols_ref, bf16[16,128,128]{2,1,0:T(8,128)(2,1)S(1)} %collective-permute-done.1.table_ref, f32[32,128]{1,0:T(8,128)S(1)} %count.1.refs_0_, ...), custom_call_target="tpu_custom_call" | custom-call | bytes 30000000 | tf_op jit(solution)/shard_map/gather_rest/pallas_call | solution.py:329
  44.9 28.2 %all_to_all.21.parts_ref = bf16[16,136,128]{2,1,0:T(8,128)(2,1)S(1)} all-to-all(bf16[16,136,128]{2,1,0:T(8,128)(2,1)S(1)} %gather_rest.1), channel_id=1, replica_groups=mesh['blk'=16,'rep'=16] {'rep'}, dimensions={0} | all-to-all | bytes 1114112 | tf_op jit(solution)/shard_map/all_to_all | solution.py:31
  73.1 2.1 %dense.1 = (bf16[256,256]{1,0:T(8,128)(2,1)}, bf16[256,128]{1,0:T(8,128)(2,1)S(1)}, bf16[16,128,128]{2,1,0:T(8,128)(2,1)}, f32[8,40,128]{2,1,0:T(8,128)S(1)}) custom-call(s32[2]{0:T(128)S(1)} %pad_add_fusion.1.place_ref, bf16[16,136,128]{2,1,0:T(8,128)(2,1)S(1)} %all_to_all.21.parts_ref, bf16[256,128]{1,0:T(8,128)(2,1)S(1)} %copy-done.1, ...), custom_call_target="tpu_custom_call" | custom-call | bytes 9000000 | tf_op jit(solution)/shard_map/dense/pallas_call | solution.py:347
  75.3 3.6 %all-to-all-start.2 = ((bf16[16,128,128]{2,1,0:T(8,128)(2,1)}), bf16[16,128,128]{2,1,0:T(8,128)(2,1)S(1)}, u32[]{:S(2)}, u32[]{:S(2)}) async-start(bf16[16,128,128]{2,1,0:T(8,128)(2,1)} %get-tuple-element.11), calls=%async_computation.2 | async-start | bytes 1048576 | tf_op jit(solution)/shard_map/all_to_all | solution.py:31
  78.9 2.6 %collective-permute-start.3 = (f32[4,40,128]{2,1,0:T(8,128)S(1)}, f32[4,40,128]{2,1,0:T(8,128)S(1)}, u32[]{:S(2)}, u32[]{:S(2)}) collective-permute-start(f32[4,40,128]{2,1,0:T(8,128)S(1)} %get-tuple-element.16), channel_id=1, source_target_pairs={{0,16},{16,0},{32,48},{48,32},{64,80},{80,64},{96,112},{112,96},{1... | collective-permute-start | bytes 245768 | tf_op jit(solution)/shard_map/ppermute | solution.py:37
  81.5 0.2 collective-permute-start.5
  81.6 1.3 collective-permute-start.4
  82.9 0.0 collective-permute-done.3
  82.9 5.0 %collective-permute-done.5 = f32[4,40,128]{2,1,0:T(8,128)S(1)} collective-permute-done((f32[4,40,128]{2,1,0:T(8,128)S(1)}, f32[4,40,128]{2,1,0:T(8,128)S(1)}, u32[]{:S(2)}, u32[]{:S(2)}) %collective-permute-start.5) | collective-permute-done | bytes 81952 | tf_op jit(solution)/shard_map/ppermute | solution.py:37
  87.9 0.7 collective-permute-done.4
  88.6 0.3 collective-permute-start.6
  88.9 1.1 collective-permute-start.8
  90.0 1.9 %collective-permute-start.7 = (f32[40,128]{1,0:T(8,128)S(1)}, f32[40,128]{1,0:T(8,128)S(1)}, u32[]{:S(2)}, u32[]{:S(2)}) collective-permute-start(f32[40,128]{1,0:T(8,128)S(1)} %get-tuple-element.20), channel_id=1, source_target_pairs={{0,128},{16,144},{32,160},{48,176},{64,192},{80,208},{96,224},{112... | collective-permute-start | bytes 61448 | tf_op jit(solution)/shard_map/ppermute | solution.py:37
  91.9 2.4 %all-to-all-done.2.table_ref = bf16[16,128,128]{2,1,0:T(8,128)(2,1)S(1)} async-done(((bf16[16,128,128]{2,1,0:T(8,128)(2,1)}), bf16[16,128,128]{2,1,0:T(8,128)(2,1)S(1)}, u32[]{:S(2)}, u32[]{:S(2)}) %all-to-all-start.2) | async-done | bytes 524320 | tf_op jit(solution)/shard_map/all_to_all | solution.py:31
  94.4 8.6 %spread_rest.1 = bf16[16,128,128]{2,1,0:T(8,128)(2,1)S(1)} custom-call(s32[2]{0:T(128)S(1)} %pad_add_fusion.1.place_ref, s32[16384]{0:T(1024)S(1)} %bitcast.51, s32[64,256]{1,0:T(8,128)S(1)} %shift_right_arithmetic.13.cols_ref, bf16[16,128,128]{2,1,0:T(8,128)(2,1)S(1)} %all-to-all-done.2.table_ref), custom_call_target="tpu_custom_call" | custom-call | bytes 27000000 | tf_op jit(solution)/shard_map/spread_rest/pallas_call | solution.py:398
  102.9 4.9 %collective-permute-start.2 = (bf16[16,128,128]{2,1,0:T(8,128)(2,1)S(1)}, bf16[16,128,128]{2,1,0:T(8,128)(2,1)S(1)}, u32[]{:S(2)}, u32[]{:S(2)}) collective-permute-start(bf16[16,128,128]{2,1,0:T(8,128)(2,1)S(1)} %spread_rest.1), channel_id=1, source_target_pairs={{0,16},{16,0},{32,48},{48,32},{64,80},{80,64},{96,112},{112,96},{1... | collective-permute-start | bytes 1572872 | tf_op jit(solution)/shard_map/ppermute | solution.py:37
  107.8 0.0 collective-permute-done.6
  107.9 0.3 collective-permute-start.11
  108.2 3.3 %collective-permute-start.10 = (f32[40,128]{1,0:T(8,128)S(1)}, f32[40,128]{1,0:T(8,128)S(1)}, u32[]{:S(2)}, u32[]{:S(2)}) collective-permute-start(f32[40,128]{1,0:T(8,128)S(1)} %fusion.2), channel_id=1, source_target_pairs={{0,8},{1,9},{2,10},{3,11},{4,12},{5,13},{6,14},{7,15},{8,0},{9,1},... | collective-permute-start | bytes 61448 | tf_op jit(solution)/shard_map/ppermute | solution.py:37
  111.5 2.1 %collective-permute-start.9 = (f32[40,128]{1,0:T(8,128)S(1)}, f32[40,128]{1,0:T(8,128)S(1)}, u32[]{:S(2)}, u32[]{:S(2)}) collective-permute-start(f32[40,128]{1,0:T(8,128)S(1)} %fusion.2), channel_id=1, source_target_pairs={{0,4},{1,5},{2,6},{3,7},{4,0},{5,1},{6,2},{7,3},{8,12},{9,13},{10,... | collective-permute-start | bytes 61448 | tf_op jit(solution)/shard_map/ppermute | solution.py:37
  113.6 1.2 collective-permute-done.10
  114.9 0.9 collective-permute-done.9
  115.8 2.0 %collective-permute-start.14 = (f32[40,128]{1,0:T(8,128)S(1)}, f32[40,128]{1,0:T(8,128)S(1)}, u32[]{:S(2)}, u32[]{:S(2)}) collective-permute-start(f32[40,128]{1,0:T(8,128)S(1)} %add_add_fusion.2), channel_id=1, source_target_pairs={{0,3},{1,2},{2,1},{3,0},{4,7},{5,6},{6,5},{7,4},{8,11},{9,10},{10,... | collective-permute-start | bytes 61448 | tf_op jit(solution)/shard_map/ppermute | solution.py:37
  117.7 0.4 collective-permute-start.13
  118.1 1.9 %collective-permute-start.12 = (f32[40,128]{1,0:T(8,128)S(1)}, f32[40,128]{1,0:T(8,128)S(1)}, u32[]{:S(2)}, u32[]{:S(2)}) collective-permute-start(f32[40,128]{1,0:T(8,128)S(1)} %add_add_fusion.2), channel_id=1, source_target_pairs={{0,1},{1,0},{2,3},{3,2},{4,5},{5,4},{6,7},{7,6},{8,9},{9,8},{10,11... | collective-permute-start | bytes 61448 | tf_op jit(solution)/shard_map/ppermute | solution.py:37
  120.0 0.9 collective-permute-done.14
  120.9 1.7 %collective-permute-done.12 = f32[40,128]{1,0:T(8,128)S(1)} collective-permute-done((f32[40,128]{1,0:T(8,128)S(1)}, f32[40,128]{1,0:T(8,128)S(1)}, u32[]{:S(2)}, u32[]{:S(2)}) %collective-permute-start.12) | collective-permute-done | bytes 20512 | tf_op jit(solution)/shard_map/ppermute | solution.py:37
  122.6 8.6 %spread_own.1.own_ref = bf16[16,128,128]{2,1,0:T(8,128)(2,1)S(1)} custom-call(s32[2]{0:T(128)S(1)} %pad_add_fusion.1.place_ref, s32[16384]{0:T(1024)S(1)} %bitcast.52, s32[64,256]{1,0:T(8,128)S(1)} %shift_right_arithmetic.13.cols_ref, bf16[16,128,128]{2,1,0:T(8,128)(2,1)S(1)} %all-to-all-done.2.table_ref), custom_call_target="tpu_custom_call" | custom-call | bytes 27000000 | tf_op jit(solution)/shard_map/spread_own/pallas_call | solution.py:398
  131.1 1.5 %join.1 = bf16[16,160,128]{2,1,0:T(8,128)(2,1)} custom-call(s32[2]{0:T(128)S(1)} %pad_add_fusion.1.place_ref, bf16[16,128,128]{2,1,0:T(8,128)(2,1)S(1)} %spread_own.1.own_ref, bf16[16,128,128]{2,1,0:T(8,128)(2,1)S(1)} %collective-permute-done.2.rest_ref, f32[40,128]{1,0:T(8,128)S(1)} %add_add_fusion.1.shares_ref), custom_call_target="tpu_custom_call" | custom-call | bytes 3000000 | tf_op jit(solution)/shard_map/join/pallas_call | solution.py:416
  132.6 3.6 %all-to-all-start.3 = ((bf16[16,160,128]{2,1,0:T(8,128)(2,1)}), bf16[16,160,128]{2,1,0:T(8,128)(2,1)S(1)}, u32[]{:S(2)}, u32[]{:S(2)}) async-start(bf16[16,160,128]{2,1,0:T(8,128)(2,1)} %join.1), calls=%async_computation.3 | async-start | bytes 1310720 | tf_op jit(solution)/shard_map/all_to_all | solution.py:31
  136.2 0.6 slice_bitcast_fusion.6
  136.8 8.7 %all-to-all-done.3.terms_ref = bf16[16,160,128]{2,1,0:T(8,128)(2,1)S(1)} async-done(((bf16[16,160,128]{2,1,0:T(8,128)(2,1)}), bf16[16,160,128]{2,1,0:T(8,128)(2,1)S(1)}, u32[]{:S(2)}, u32[]{:S(2)}) %all-to-all-start.3) | async-done | bytes 655392 | tf_op jit(solution)/shard_map/all_to_all | solution.py:31
  145.5 0.8 close.1
  (28 shorter events, 0.3 us)
Async XLA Ops:
  0.6 20.4 %copy-start.5 = (s32[1,16,2,256]{3,2,1,0:T(2,128)S(1)}, s32[1,16,2,256]{3,2,1,0:T(2,128)}, u32[]{:S(2)}) copy-start(s32[1,16,2,256]{3,2,1,0:T(2,128)} %param.8) | copy-start | bytes 98308
  0.6 20.4 %copy-start.6 = (s32[1,16,2,256]{3,2,1,0:T(2,128)S(1)}, s32[1,16,2,256]{3,2,1,0:T(2,128)}, u32[]{:S(2)}) copy-start(s32[1,16,2,256]{3,2,1,0:T(2,128)} %param.9) | copy-start | bytes 98308
  18.3 16.1 %collective-permute-start.1 = (bf16[16,128,128]{2,1,0:T(8,128)(2,1)S(1)}, bf16[16,128,128]{2,1,0:T(8,128)(2,1)S(1)}, u32[]{:S(2)}, u32[]{:S(2)}) collective-permute-start(bf16[16,128,128]{2,1,0:T(8,128)(2,1)S(1)} %all_to_all.20.table_ref), channel_id=1, source_target_pairs={{0,16},{16,0},{32,48},{48,32},{64,80},{80,64},{96,112},{112,96},{1... | collective-permute-start | bytes 1572872 | tf_op jit(solution)/shard_map/ppermute | solution.py:37
  21.0 4.4 %collective-permute-start = (s32[16,2,256]{2,1,0:T(2,128)S(1)}, s32[16,2,256]{2,1,0:T(2,128)S(1)}, u32[]{:S(2)}, u32[]{:S(2)}) collective-permute-start(s32[16,2,256]{2,1,0:T(2,128)S(1)} %or_bitcast_fusion), channel_id=1, source_target_pairs={{0,1},{1,0},{2,3},{3,2},{4,5},{5,4},{6,7},{7,6},{8,9},{9,8},{10,11... | collective-permute-start | bytes 98312 | tf_op jit(solution)/shard_map/ppermute | solution.py:37
  34.3 38.8 %copy-start = (bf16[4096,256]{1,0:T(8,128)(2,1)S(1)}, bf16[4096,256]{1,0:T(8,128)(2,1)}, u32[]{:S(2)}) copy-start(bf16[4096,256]{1,0:T(8,128)(2,1)} %upstream_ref.1) | copy-start | bytes 6291460
  34.3 38.8 %copy-start.1 = (bf16[256,128]{1,0:T(8,128)(2,1)S(1)}, bf16[256,128]{1,0:T(8,128)(2,1)}, u32[]{:S(2)}) copy-start(bf16[256,128]{1,0:T(8,128)(2,1)} %feats_ref.1) | copy-start | bytes 196612
  34.3 38.8 %copy-start.2 = (bf16[128,256]{1,0:T(8,128)(2,1)S(1)}, bf16[128,256]{1,0:T(8,128)(2,1)}, u32[]{:S(2)}) copy-start(bf16[128,256]{1,0:T(8,128)(2,1)} %weight_ref.1) | copy-start | bytes 196612
  34.3 38.8 %copy-start.3 = (s32[4096]{0:T(1024)S(1)}, s32[4096]{0:T(1024)}, u32[]{:S(2)}) copy-start(s32[4096]{0:T(1024)} %param.13) | copy-start | bytes 49156
  34.3 38.8 %copy-start.4 = (f32[256]{0:T(256)S(1)}, f32[256]{0:T(256)}, u32[]{:S(2)}) copy-start(f32[256]{0:T(256)} %param.11) | copy-start | bytes 3076
  75.3 19.1 %all-to-all-start.2 = ((bf16[16,128,128]{2,1,0:T(8,128)(2,1)}), bf16[16,128,128]{2,1,0:T(8,128)(2,1)S(1)}, u32[]{:S(2)}, u32[]{:S(2)}) async-start(bf16[16,128,128]{2,1,0:T(8,128)(2,1)} %get-tuple-element.11), calls=%async_computation.2 | async-start | bytes 1048576 | tf_op jit(solution)/shard_map/all_to_all | solution.py:31
  78.9 4.0 %collective-permute-start.3 = (f32[4,40,128]{2,1,0:T(8,128)S(1)}, f32[4,40,128]{2,1,0:T(8,128)S(1)}, u32[]{:S(2)}, u32[]{:S(2)}) collective-permute-start(f32[4,40,128]{2,1,0:T(8,128)S(1)} %get-tuple-element.16), channel_id=1, source_target_pairs={{0,16},{16,0},{32,48},{48,32},{64,80},{80,64},{96,112},{112,96},{1... | collective-permute-start | bytes 245768 | tf_op jit(solution)/shard_map/ppermute | solution.py:37
  81.5 6.4 %collective-permute-start.5 = (f32[4,40,128]{2,1,0:T(8,128)S(1)}, f32[4,40,128]{2,1,0:T(8,128)S(1)}, u32[]{:S(2)}, u32[]{:S(2)}) collective-permute-start(f32[4,40,128]{2,1,0:T(8,128)S(1)} %get-tuple-element.17), channel_id=1, source_target_pairs={{0,48},{16,32},{32,16},{48,0},{64,112},{80,96},{96,80},{112,64},{1... | collective-permute-start | bytes 245768 | tf_op jit(solution)/shard_map/ppermute | solution.py:37
  81.6 6.9 %collective-permute-start.4 = (f32[4,40,128]{2,1,0:T(8,128)S(1)}, f32[4,40,128]{2,1,0:T(8,128)S(1)}, u32[]{:S(2)}, u32[]{:S(2)}) collective-permute-start(f32[4,40,128]{2,1,0:T(8,128)S(1)} %get-tuple-element.17), channel_id=1, source_target_pairs={{0,32},{16,48},{32,0},{48,16},{64,96},{80,112},{96,64},{112,80},{1... | collective-permute-start | bytes 245768 | tf_op jit(solution)/shard_map/ppermute | solution.py:37
  88.6 19.2 %collective-permute-start.6 = (f32[40,128]{1,0:T(8,128)S(1)}, f32[40,128]{1,0:T(8,128)S(1)}, u32[]{:S(2)}, u32[]{:S(2)}) collective-permute-start(f32[40,128]{1,0:T(8,128)S(1)} %get-tuple-element.18), channel_id=1, source_target_pairs={{0,64},{16,80},{32,96},{48,112},{64,0},{80,16},{96,32},{112,48},{1... | collective-permute-start | bytes 61448 | tf_op jit(solution)/shard_map/ppermute | solution.py:37
  88.9 18.9 %collective-permute-start.8 = (f32[40,128]{1,0:T(8,128)S(1)}, f32[40,128]{1,0:T(8,128)S(1)}, u32[]{:S(2)}, u32[]{:S(2)}) collective-permute-start(f32[40,128]{1,0:T(8,128)S(1)} %get-tuple-element.19), channel_id=1, source_target_pairs={{0,192},{16,208},{32,224},{48,240},{64,128},{80,144},{96,160},{112... | collective-permute-start | bytes 61448 | tf_op jit(solution)/shard_map/ppermute | solution.py:37
  90.0 17.8 %collective-permute-start.7 = (f32[40,128]{1,0:T(8,128)S(1)}, f32[40,128]{1,0:T(8,128)S(1)}, u32[]{:S(2)}, u32[]{:S(2)}) collective-permute-start(f32[40,128]{1,0:T(8,128)S(1)} %get-tuple-element.20), channel_id=1, source_target_pairs={{0,128},{16,144},{32,160},{48,176},{64,192},{80,208},{96,224},{112... | collective-permute-start | bytes 61448 | tf_op jit(solution)/shard_map/ppermute | solution.py:37
  102.9 28.2 %collective-permute-start.2 = (bf16[16,128,128]{2,1,0:T(8,128)(2,1)S(1)}, bf16[16,128,128]{2,1,0:T(8,128)(2,1)S(1)}, u32[]{:S(2)}, u32[]{:S(2)}) collective-permute-start(bf16[16,128,128]{2,1,0:T(8,128)(2,1)S(1)} %spread_rest.1), channel_id=1, source_target_pairs={{0,16},{16,0},{32,48},{48,32},{64,80},{80,64},{96,112},{112,96},{1... | collective-permute-start | bytes 1572872 | tf_op jit(solution)/shard_map/ppermute | solution.py:37
  107.9 5.7 %collective-permute-start.11 = (f32[40,128]{1,0:T(8,128)S(1)}, f32[40,128]{1,0:T(8,128)S(1)}, u32[]{:S(2)}, u32[]{:S(2)}) collective-permute-start(f32[40,128]{1,0:T(8,128)S(1)} %fusion.2), channel_id=1, source_target_pairs={{0,12},{1,13},{2,14},{3,15},{4,8},{5,9},{6,10},{7,11},{8,4},{9,5},... | collective-permute-start | bytes 61448 | tf_op jit(solution)/shard_map/ppermute | solution.py:37
  108.2 6.6 %collective-permute-start.10 = (f32[40,128]{1,0:T(8,128)S(1)}, f32[40,128]{1,0:T(8,128)S(1)}, u32[]{:S(2)}, u32[]{:S(2)}) collective-permute-start(f32[40,128]{1,0:T(8,128)S(1)} %fusion.2), channel_id=1, source_target_pairs={{0,8},{1,9},{2,10},{3,11},{4,12},{5,13},{6,14},{7,15},{8,0},{9,1},... | collective-permute-start | bytes 61448 | tf_op jit(solution)/shard_map/ppermute | solution.py:37
  111.5 4.2 %collective-permute-start.9 = (f32[40,128]{1,0:T(8,128)S(1)}, f32[40,128]{1,0:T(8,128)S(1)}, u32[]{:S(2)}, u32[]{:S(2)}) collective-permute-start(f32[40,128]{1,0:T(8,128)S(1)} %fusion.2), channel_id=1, source_target_pairs={{0,4},{1,5},{2,6},{3,7},{4,0},{5,1},{6,2},{7,3},{8,12},{9,13},{10,... | collective-permute-start | bytes 61448 | tf_op jit(solution)/shard_map/ppermute | solution.py:37
  115.8 5.1 %collective-permute-start.14 = (f32[40,128]{1,0:T(8,128)S(1)}, f32[40,128]{1,0:T(8,128)S(1)}, u32[]{:S(2)}, u32[]{:S(2)}) collective-permute-start(f32[40,128]{1,0:T(8,128)S(1)} %add_add_fusion.2), channel_id=1, source_target_pairs={{0,3},{1,2},{2,1},{3,0},{4,7},{5,6},{6,5},{7,4},{8,11},{9,10},{10,... | collective-permute-start | bytes 61448 | tf_op jit(solution)/shard_map/ppermute | solution.py:37
  117.7 3.1 %collective-permute-start.13 = (f32[40,128]{1,0:T(8,128)S(1)}, f32[40,128]{1,0:T(8,128)S(1)}, u32[]{:S(2)}, u32[]{:S(2)}) collective-permute-start(f32[40,128]{1,0:T(8,128)S(1)} %add_add_fusion.2), channel_id=1, source_target_pairs={{0,2},{1,3},{2,0},{3,1},{4,6},{5,7},{6,4},{7,5},{8,10},{9,11},{10,... | collective-permute-start | bytes 61448 | tf_op jit(solution)/shard_map/ppermute | solution.py:37
  118.1 4.4 %collective-permute-start.12 = (f32[40,128]{1,0:T(8,128)S(1)}, f32[40,128]{1,0:T(8,128)S(1)}, u32[]{:S(2)}, u32[]{:S(2)}) collective-permute-start(f32[40,128]{1,0:T(8,128)S(1)} %add_add_fusion.2), channel_id=1, source_target_pairs={{0,1},{1,0},{2,3},{3,2},{4,5},{5,4},{6,7},{7,6},{8,9},{9,8},{10,11... | collective-permute-start | bytes 61448 | tf_op jit(solution)/shard_map/ppermute | solution.py:37
  132.6 12.9 %all-to-all-start.3 = ((bf16[16,160,128]{2,1,0:T(8,128)(2,1)}), bf16[16,160,128]{2,1,0:T(8,128)(2,1)S(1)}, u32[]{:S(2)}, u32[]{:S(2)}) async-start(bf16[16,160,128]{2,1,0:T(8,128)(2,1)} %join.1), calls=%async_computation.3 | async-start | bytes 1310720 | tf_op jit(solution)/shard_map/all_to_all | solution.py:31

commit v5 on v4

--- a/solution.py
+++ b/solution.py
@@ -16,7 +16,7 @@
 TN = (((0,), (0,)), ((), ()))
 NT = (((1,), (1,)), ((), ()))
 TOTALS = 8
-CHUNK = 1024
+CHUNK = 2048
 
 VMEM = pl.BlockSpec(memory_space=pltpu.VMEM)
 ANY = pl.BlockSpec(memory_space=pl.ANY)
@@ -77,12 +77,10 @@
 
 def gather_sum_kernel(closing, place_ref, rows_ref, cols_ref, table_ref, *refs):
     if closing:
-        counts_ref, before_ref, out_ref, list0, list1, sems, values0, values1, held_ref, sem = refs[:10]
-        totals = refs[10:]
-        pltpu.make_async_copy(before_ref, held_ref, sem).start()
-    else:
-        out_ref, list0, list1, sems, values0, values1 = refs[:6]
-        totals = refs[6:]
+        counts_ref, refs = refs[0], refs[1 + TOTALS :]
+        out_ref, refs = refs[0], refs[1:]
+    totals, refs = refs[:TOTALS], refs[TOTALS:]
+    list0, list1, sems, values0, values1 = refs
     lists, values = (list0, list1), (values0, values1)
     slots = cols_ref.shape[1]
     blocks = cols_ref.shape[0] // 2
@@ -105,8 +103,9 @@
 
     for side in range(2):
         fetch(side, side).start()
-    for total in totals:
-        total[...] = jnp.zeros_like(total)
+    if not closing:
+        for total in totals:
+            total[...] = jnp.zeros_like(total)
     pick(0, 0)
 
     @pl.loop(0, steps)
@@ -126,10 +125,10 @@
             def _():
                 fetch(2 * i + side + 2, side).start()
 
+    if not closing:
+        return
     piece_rows = 2 * CB
     left = left_lanes(CB)
-    if closing:
-        pltpu.make_async_copy(before_ref, held_ref, sem).wait()
 
     @pl.loop(0, totals[0].shape[0] // piece_rows)
     def _(p):
@@ -137,10 +136,6 @@
         part = totals[0][span, :]
         for total in totals[1:]:
             part += total[span, :]
-        if not closing:
-            out_ref[span, :] = part
-            return
-        part += held_ref[span, :]
         part += turned(part)
         out_ref[p, :CB, :] = jnp.where(left, part[:CB], part[CB:]).astype(BF)
         groups = piece_rows // LANES
@@ -310,35 +305,34 @@
         out_shape=jax.ShapeDtypeStruct((panel_rows // LANES, LANES), F32),
         cost_estimate=cost(2),
         compiler_params=pltpu.CompilerParams(vmem_limit_bytes=8 << 20),
-    name="count",
+        name="count",
     )(own_rows)
     chunks = [pltpu.SMEM((CHUNK,), jnp.int32)] * 2 + [pltpu.SemaphoreType.DMA((2,))]
 
     whole_panel = pltpu.VMEM((panel_rows, width), F32)
     values = [pltpu.VMEM((slots, width), F32)] * 2
-    partial = pl.pallas_call(
+    total = jax.ShapeDtypeStruct((panel_rows, width), F32)
+    totals = pl.pallas_call(
         functools.partial(gather_sum_kernel, False),
         in_specs=[SMEM, ANY, VMEM, VMEM],
-        out_specs=VMEM,
-        out_shape=jax.ShapeDtypeStruct((panel_rows, width), F32),
-        scratch_shapes=chunks + values + [whole_panel] * TOTALS,
+        out_specs=[VMEM] * TOTALS,
+        out_shape=[total] * TOTALS,
+        scratch_shapes=chunks + values,
         cost_estimate=cost(10),
-        compiler_params=pltpu.CompilerParams(vmem_limit_bytes=26 << 20),
+        compiler_params=pltpu.CompilerParams(vmem_limit_bytes=20 << 20),
         name="gather_own",
     )(places, row_list, cols, table)
-    sends = pl.pallas_call(
+    sends, *_ = pl.pallas_call(
         functools.partial(gather_sum_kernel, True),
-        in_specs=[SMEM, ANY, VMEM, VMEM, VMEM, ANY],
-        out_specs=VMEM,
-        out_shape=jax.ShapeDtypeStruct((n_rep, half + 8, width), BF),
-        scratch_shapes=chunks
-        + values
-        + [whole_panel, pltpu.SemaphoreType.DMA]
-        + [whole_panel] * TOTALS,
+        in_specs=[SMEM, ANY, VMEM, VMEM, VMEM] + [VMEM] * TOTALS,
+        out_specs=[VMEM] * (1 + TOTALS),
+        out_shape=[jax.ShapeDtypeStruct((n_rep, half + 8, width), BF)] + [total] * TOTALS,
+        scratch_shapes=chunks + values,
+        input_output_aliases={5 + j: 1 + j for j in range(TOTALS)},
         cost_estimate=cost(10),
-        compiler_params=pltpu.CompilerParams(vmem_limit_bytes=28 << 20),
+        compiler_params=pltpu.CompilerParams(vmem_limit_bytes=20 << 20),
         name="gather_rest",
-    )(places, row_list, cols, other_table, counts, partial)
+    )(places, row_list, cols, other_table, counts, *totals)
     parts = exchange(sends, "rep")
 
     share = width // (n_blk // 2)

time: 149 us -> 145 us (0.973)
  Pallas kernels: 41.6 us -> 37.9 us
  transfers between devices with their start and end apart: 17 -> 17, of which waited for: 9 -> 9; matrix products, arithmetic and copies ran while one was open for 1% -> 1% of each run, Pallas kernels for 18% -> 17%
where the time goes in v5:
time: 145 us; the launch traced here: 143 us
  blocking collectives  44.7 us (31%)
  Pallas kernels  37.9 us (26%)
  starting transfers between devices  33.7 us (23%)
  waiting for transfers between devices  23.4 us (16%)
  local copies, waits for them, and re-layouts  1.75 us (1%)
    all_to_all x2, blocking collectives, exchange(): lax.all_to_all(parts, axis, split_axis=0, concat_axis=0, tiled=True, axis...  44.7 us
    ppermute x15, starting transfers between devices, swapped(): return lax.ppermute(value, axis, [(i, i ^ bits) for i in range(count)])  26.6 us
    pallas_call x2, Pallas kernels, spread(): pl.pallas_call(functools.partial(spread_kernel, own), in_specs=[SMEM, ANY...  15.8 us
    ppermute x15, waiting for transfers between devices, swapped(): return lax.ppermute(value, axis, [(i, i ^ bits) for i in range(count)])  12.2 us
    all_to_all x2, waiting for transfers between devices, exchange(): lax.all_to_all(parts, axis, split_axis=0, concat_axis=0, tiled=True, axis...  11.2 us
    pallas_call x1, Pallas kernels, layer(): pl.pallas_call(functools.partial(gather_sum_kernel, True), in_specs=[SMEM...  9.14 us
    pallas_call x1, Pallas kernels, layer(): pl.pallas_call(functools.partial(gather_sum_kernel, False), in_specs=[SME...  7.76 us
    all_to_all x2, starting transfers between devices, exchange(): lax.all_to_all(parts, axis, split_axis=0, concat_axis=0, tiled=True, axis...  7.16 us
  transfers between devices with their start and end apart: 17, of which 9 were waited for; matrix products, arithmetic and copies ran while one was open for 1% of the time, Pallas kernels for 17%

profile of v5, /device:TPU:1, one launch (start us, length us, event | category | flops | bytes accessed | tf_op | source)
XLA Modules:
  0.0 142.7 jit_solution(15850708835533177855)
XLA Ops:
  0.7 0.9 fusion.3
  1.6 0.1 maximum_bitcast_fusion
  1.7 0.1 broadcast_in_dim.3
  1.8 16.5 %all_to_all.20.table_ref = bf16[16,128,128]{2,1,0:T(8,128)(2,1)S(1)} all-to-all(bf16[16,128,128]{2,1,0:T(8,128)(2,1)S(1)} %bitcast.57), channel_id=1, replica_groups={{0,1,32,33,64,65,96,97,128,129,160,161,192,193,224,225},{2,3,34,35,66,6..., dimensions={0} | all-to-all | bytes 1048576 | tf_op jit(solution)/shard_map/all_to_all | solution.py:31
  18.3 2.7 %collective-permute-start.1 = (bf16[16,128,128]{2,1,0:T(8,128)(2,1)S(1)}, bf16[16,128,128]{2,1,0:T(8,128)(2,1)S(1)}, u32[]{:S(2)}, u32[]{:S(2)}) collective-permute-start(bf16[16,128,128]{2,1,0:T(8,128)(2,1)S(1)} %all_to_all.20.table_ref), channel_id=1, source_target_pairs={{0,16},{16,0},{32,48},{48,32},{64,80},{80,64},{96,112},{112,96},{1... | collective-permute-start | bytes 1572872 | tf_op jit(solution)/shard_map/ppermute | solution.py:37
  21.0 1.6 %collective-permute-start = (s32[16,2,256]{2,1,0:T(2,128)S(1)}, s32[16,2,256]{2,1,0:T(2,128)S(1)}, u32[]{:S(2)}, u32[]{:S(2)}) collective-permute-start(s32[16,2,256]{2,1,0:T(2,128)S(1)} %or_bitcast_fusion), channel_id=1, source_target_pairs={{0,1},{1,0},{2,3},{3,2},{4,5},{5,4},{6,7},{7,6},{8,9},{9,8},{10,11... | collective-permute-start | bytes 98312 | tf_op jit(solution)/shard_map/ppermute | solution.py:37
  22.6 0.1 pad_add_fusion.1.place_ref
  22.7 0.8 count.1.refs_0_
  23.5 1.8 %collective-permute-done = s32[16,2,256]{2,1,0:T(2,128)S(1)} collective-permute-done((s32[16,2,256]{2,1,0:T(2,128)S(1)}, s32[16,2,256]{2,1,0:T(2,128)S(1)}, u32[]{:S(2)}, u32[]{:S(2)}) %collective-permute-start) | collective-permute-done | bytes 32800 | tf_op jit(solution)/shard_map/ppermute | solution.py:37
  25.5 7.8 %gather_own.1 = (f32[4096,128]{1,0:T(8,128)S(1)}, f32[4096,128]{1,0:T(8,128)S(1)}, f32[4096,128]{1,0:T(8,128)S(1)}, f32[4096,128]{1,0:T(8,128)S(1)}, f32[4096,12...) custom-call(s32[2]{0:T(128)S(1)} %pad_add_fusion.1.place_ref, ...), custom_call_target="tpu_custom_call" | custom-call | bytes 30000000 | tf_op jit(solution)/shard_map/gather_own/pallas_call | solution.py:315
  33.3 0.0 collective-permute-done.1.table_ref
  33.3 0.0 copy-start
  33.3 0.0 copy-start.1
  33.3 0.0 copy-start.2
  33.4 0.0 copy-start.3
  33.4 0.0 copy-start.4
  33.4 9.1 %gather_rest.1 = (bf16[16,136,128]{2,1,0:T(8,128)(2,1)S(1)}, f32[4096,128]{1,0:T(8,128)S(1)}, f32[4096,128]{1,0:T(8,128)S(1)}, f32[4096,128]{1,0:T(8,128)S(1)}, ...) custom-call(s32[2]{0:T(128)S(1)} %pad_add_fusion.1.place_ref, ...), custom_call_target="tpu_custom_call", output_to_operand_aliasing={{1}: (5, {}), {2}: (6, {}), {3}: (7, {}), {4}: (8, {}), {5}... | custom-call | bytes 30000000 | tf_op jit(solution)/shard_map/gather_rest/pallas_call | solution.py:325
  42.5 28.2 %all_to_all.21.parts_ref = bf16[16,136,128]{2,1,0:T(8,128)(2,1)S(1)} all-to-all(bf16[16,136,128]{2,1,0:T(8,128)(2,1)S(1)} %get-tuple-element.27), channel_id=1, replica_groups=mesh['blk'=16,'rep'=16] {'rep'}, dimensions={0} | all-to-all | bytes 1114112 | tf_op jit(solution)/shard_map/all_to_all | solution.py:31
  70.8 2.1 %dense.1 = (bf16[256,256]{1,0:T(8,128)(2,1)}, bf16[256,128]{1,0:T(8,128)(2,1)S(1)}, bf16[16,128,128]{2,1,0:T(8,128)(2,1)}, f32[8,40,128]{2,1,0:T(8,128)S(1)}) custom-call(s32[2]{0:T(128)S(1)} %pad_add_fusion.1.place_ref, bf16[16,136,128]{2,1,0:T(8,128)(2,1)S(1)} %all_to_all.21.parts_ref, bf16[256,128]{1,0:T(8,128)(2,1)S(1)} %copy-done.1, ...), custom_call_target="tpu_custom_call" | custom-call | bytes 9000000 | tf_op jit(solution)/shard_map/dense/pallas_call | solution.py:341
  72.9 3.6 %all-to-all-start.2 = ((bf16[16,128,128]{2,1,0:T(8,128)(2,1)}), bf16[16,128,128]{2,1,0:T(8,128)(2,1)S(1)}, u32[]{:S(2)}, u32[]{:S(2)}) async-start(bf16[16,128,128]{2,1,0:T(8,128)(2,1)} %get-tuple-element.29), calls=%async_computation.2 | async-start | bytes 1048576 | tf_op jit(solution)/shard_map/all_to_all | solution.py:31
  76.5 2.6 %collective-permute-start.3 = (f32[4,40,128]{2,1,0:T(8,128)S(1)}, f32[4,40,128]{2,1,0:T(8,128)S(1)}, u32[]{:S(2)}, u32[]{:S(2)}) collective-permute-start(f32[4,40,128]{2,1,0:T(8,128)S(1)} %get-tuple-element.34), channel_id=1, source_target_pairs={{0,16},{16,0},{32,48},{48,32},{64,80},{80,64},{96,112},{112,96},{1... | collective-permute-start | bytes 245768 | tf_op jit(solution)/shard_map/ppermute | solution.py:37
  79.1 0.2 collective-permute-start.5
  79.2 1.3 collective-permute-start.4
  80.5 0.0 collective-permute-done.3
  80.6 5.0 %collective-permute-done.5 = f32[4,40,128]{2,1,0:T(8,128)S(1)} collective-permute-done((f32[4,40,128]{2,1,0:T(8,128)S(1)}, f32[4,40,128]{2,1,0:T(8,128)S(1)}, u32[]{:S(2)}, u32[]{:S(2)}) %collective-permute-start.5) | collective-permute-done | bytes 81952 | tf_op jit(solution)/shard_map/ppermute | solution.py:37
  85.5 0.7 collective-permute-done.4
  86.2 0.3 collective-permute-start.6
  86.6 1.1 collective-permute-start.8
  87.6 1.9 %collective-permute-start.7 = (f32[40,128]{1,0:T(8,128)S(1)}, f32[40,128]{1,0:T(8,128)S(1)}, u32[]{:S(2)}, u32[]{:S(2)}) collective-permute-start(f32[40,128]{1,0:T(8,128)S(1)} %get-tuple-element.38), channel_id=1, source_target_pairs={{0,128},{16,144},{32,160},{48,176},{64,192},{80,208},{96,224},{112... | collective-permute-start | bytes 61448 | tf_op jit(solution)/shard_map/ppermute | solution.py:37
  89.6 2.4 %all-to-all-done.2.table_ref = bf16[16,128,128]{2,1,0:T(8,128)(2,1)S(1)} async-done(((bf16[16,128,128]{2,1,0:T(8,128)(2,1)}), bf16[16,128,128]{2,1,0:T(8,128)(2,1)S(1)}, u32[]{:S(2)}, u32[]{:S(2)}) %all-to-all-start.2) | async-done | bytes 524320 | tf_op jit(solution)/shard_map/all_to_all | solution.py:31
  92.0 7.9 %spread_rest.1 = bf16[16,128,128]{2,1,0:T(8,128)(2,1)S(1)} custom-call(s32[2]{0:T(128)S(1)} %pad_add_fusion.1.place_ref, s32[16384]{0:T(1024)S(1)} %bitcast.51, s32[64,256]{1,0:T(8,128)S(1)} %shift_right_arithmetic.13.cols_ref, bf16[16,128,128]{2,1,0:T(8,128)(2,1)S(1)} %all-to-all-done.2.table_ref), custom_call_target="tpu_custom_call" | custom-call | bytes 27000000 | tf_op jit(solution)/shard_map/spread_rest/pallas_call | solution.py:392
  99.9 4.9 %collective-permute-start.2 = (bf16[16,128,128]{2,1,0:T(8,128)(2,1)S(1)}, bf16[16,128,128]{2,1,0:T(8,128)(2,1)S(1)}, u32[]{:S(2)}, u32[]{:S(2)}) collective-permute-start(bf16[16,128,128]{2,1,0:T(8,128)(2,1)S(1)} %spread_rest.1), channel_id=1, source_target_pairs={{0,16},{16,0},{32,48},{48,32},{64,80},{80,64},{96,112},{112,96},{1... | collective-permute-start | bytes 1572872 | tf_op jit(solution)/shard_map/ppermute | solution.py:37
  104.8 0.3 collective-permute-start.11
  105.2 3.3 %collective-permute-start.10 = (f32[40,128]{1,0:T(8,128)S(1)}, f32[40,128]{1,0:T(8,128)S(1)}, u32[]{:S(2)}, u32[]{:S(2)}) collective-permute-start(f32[40,128]{1,0:T(8,128)S(1)} %fusion.2), channel_id=1, source_target_pairs={{0,8},{1,9},{2,10},{3,11},{4,12},{5,13},{6,14},{7,15},{8,0},{9,1},... | collective-permute-start | bytes 61448 | tf_op jit(solution)/shard_map/ppermute | solution.py:37
  108.5 2.1 %collective-permute-start.9 = (f32[40,128]{1,0:T(8,128)S(1)}, f32[40,128]{1,0:T(8,128)S(1)}, u32[]{:S(2)}, u32[]{:S(2)}) collective-permute-start(f32[40,128]{1,0:T(8,128)S(1)} %fusion.2), channel_id=1, source_target_pairs={{0,4},{1,5},{2,6},{3,7},{4,0},{5,1},{6,2},{7,3},{8,12},{9,13},{10,... | collective-permute-start | bytes 61448 | tf_op jit(solution)/shard_map/ppermute | solution.py:37
  110.6 1.3 collective-permute-done.10
  111.9 0.9 collective-permute-done.9
  112.8 2.1 %collective-permute-start.14 = (f32[40,128]{1,0:T(8,128)S(1)}, f32[40,128]{1,0:T(8,128)S(1)}, u32[]{:S(2)}, u32[]{:S(2)}) collective-permute-start(f32[40,128]{1,0:T(8,128)S(1)} %add_add_fusion.2), channel_id=1, source_target_pairs={{0,3},{1,2},{2,1},{3,0},{4,7},{5,6},{6,5},{7,4},{8,11},{9,10},{10,... | collective-permute-start | bytes 61448 | tf_op jit(solution)/shard_map/ppermute | solution.py:37
  114.9 0.2 collective-permute-start.13
  115.1 1.9 %collective-permute-start.12 = (f32[40,128]{1,0:T(8,128)S(1)}, f32[40,128]{1,0:T(8,128)S(1)}, u32[]{:S(2)}, u32[]{:S(2)}) collective-permute-start(f32[40,128]{1,0:T(8,128)S(1)} %add_add_fusion.2), channel_id=1, source_target_pairs={{0,1},{1,0},{2,3},{3,2},{4,5},{5,4},{6,7},{7,6},{8,9},{9,8},{10,11... | collective-permute-start | bytes 61448 | tf_op jit(solution)/shard_map/ppermute | solution.py:37
  117.0 0.9 collective-permute-done.14
  117.9 1.6 %collective-permute-done.12 = f32[40,128]{1,0:T(8,128)S(1)} collective-permute-done((f32[40,128]{1,0:T(8,128)S(1)}, f32[40,128]{1,0:T(8,128)S(1)}, u32[]{:S(2)}, u32[]{:S(2)}) %collective-permute-start.12) | collective-permute-done | bytes 20512 | tf_op jit(solution)/shard_map/ppermute | solution.py:37
  119.5 7.9 %spread_own.1.own_ref = bf16[16,128,128]{2,1,0:T(8,128)(2,1)S(1)} custom-call(s32[2]{0:T(128)S(1)} %pad_add_fusion.1.place_ref, s32[16384]{0:T(1024)S(1)} %bitcast.52, s32[64,256]{1,0:T(8,128)S(1)} %shift_right_arithmetic.13.cols_ref, bf16[16,128,128]{2,1,0:T(8,128)(2,1)S(1)} %all-to-all-done.2.table_ref), custom_call_target="tpu_custom_call" | custom-call | bytes 27000000 | tf_op jit(solution)/shard_map/spread_own/pallas_call | solution.py:392
  127.5 1.5 %join.1 = bf16[16,160,128]{2,1,0:T(8,128)(2,1)} custom-call(s32[2]{0:T(128)S(1)} %pad_add_fusion.1.place_ref, bf16[16,128,128]{2,1,0:T(8,128)(2,1)S(1)} %spread_own.1.own_ref, bf16[16,128,128]{2,1,0:T(8,128)(2,1)S(1)} %collective-permute-done.2.rest_ref, f32[40,128]{1,0:T(8,128)S(1)} %add_add_fusion.1.shares_ref), custom_call_target="tpu_custom_call" | custom-call | bytes 3000000 | tf_op jit(solution)/shard_map/join/pallas_call | solution.py:410
  129.0 3.6 %all-to-all-start.3 = ((bf16[16,160,128]{2,1,0:T(8,128)(2,1)}), bf16[16,160,128]{2,1,0:T(8,128)(2,1)S(1)}, u32[]{:S(2)}, u32[]{:S(2)}) async-start(bf16[16,160,128]{2,1,0:T(8,128)(2,1)} %join.1), calls=%async_computation.3 | async-start | bytes 1310720 | tf_op jit(solution)/shard_map/all_to_all | solution.py:31
  132.6 0.6 slice_bitcast_fusion.6
  133.2 8.8 %all-to-all-done.3.terms_ref = bf16[16,160,128]{2,1,0:T(8,128)(2,1)S(1)} async-done(((bf16[16,160,128]{2,1,0:T(8,128)(2,1)}), bf16[16,160,128]{2,1,0:T(8,128)(2,1)S(1)}, u32[]{:S(2)}, u32[]{:S(2)}) %all-to-all-start.3) | async-done | bytes 655392 | tf_op jit(solution)/shard_map/all_to_all | solution.py:31
  141.9 0.8 close.1
  (28 shorter events, 0.3 us)
Async XLA Ops:
  0.6 20.4 %copy-start.5 = (s32[1,16,2,256]{3,2,1,0:T(2,128)S(1)}, s32[1,16,2,256]{3,2,1,0:T(2,128)}, u32[]{:S(2)}) copy-start(s32[1,16,2,256]{3,2,1,0:T(2,128)} %param.8) | copy-start | bytes 98308
  0.6 20.4 %copy-start.6 = (s32[1,16,2,256]{3,2,1,0:T(2,128)S(1)}, s32[1,16,2,256]{3,2,1,0:T(2,128)}, u32[]{:S(2)}) copy-start(s32[1,16,2,256]{3,2,1,0:T(2,128)} %param.9) | copy-start | bytes 98308
  18.3 15.0 %collective-permute-start.1 = (bf16[16,128,128]{2,1,0:T(8,128)(2,1)S(1)}, bf16[16,128,128]{2,1,0:T(8,128)(2,1)S(1)}, u32[]{:S(2)}, u32[]{:S(2)}) collective-permute-start(bf16[16,128,128]{2,1,0:T(8,128)(2,1)S(1)} %all_to_all.20.table_ref), channel_id=1, source_target_pairs={{0,16},{16,0},{32,48},{48,32},{64,80},{80,64},{96,112},{112,96},{1... | collective-permute-start | bytes 1572872 | tf_op jit(solution)/shard_map/ppermute | solution.py:37
  21.0 4.4 %collective-permute-start = (s32[16,2,256]{2,1,0:T(2,128)S(1)}, s32[16,2,256]{2,1,0:T(2,128)S(1)}, u32[]{:S(2)}, u32[]{:S(2)}) collective-permute-start(s32[16,2,256]{2,1,0:T(2,128)S(1)} %or_bitcast_fusion), channel_id=1, source_target_pairs={{0,1},{1,0},{2,3},{3,2},{4,5},{5,4},{6,7},{7,6},{8,9},{9,8},{10,11... | collective-permute-start | bytes 98312 | tf_op jit(solution)/shard_map/ppermute | solution.py:37
  33.3 37.4 %copy-start = (bf16[4096,256]{1,0:T(8,128)(2,1)S(1)}, bf16[4096,256]{1,0:T(8,128)(2,1)}, u32[]{:S(2)}) copy-start(bf16[4096,256]{1,0:T(8,128)(2,1)} %upstream_ref.1) | copy-start | bytes 6291460
  33.3 37.4 %copy-start.1 = (bf16[256,128]{1,0:T(8,128)(2,1)S(1)}, bf16[256,128]{1,0:T(8,128)(2,1)}, u32[]{:S(2)}) copy-start(bf16[256,128]{1,0:T(8,128)(2,1)} %feats_ref.1) | copy-start | bytes 196612
  33.3 37.4 %copy-start.2 = (bf16[128,256]{1,0:T(8,128)(2,1)S(1)}, bf16[128,256]{1,0:T(8,128)(2,1)}, u32[]{:S(2)}) copy-start(bf16[128,256]{1,0:T(8,128)(2,1)} %weight_ref.1) | copy-start | bytes 196612
  33.4 37.4 %copy-start.3 = (s32[4096]{0:T(1024)S(1)}, s32[4096]{0:T(1024)}, u32[]{:S(2)}) copy-start(s32[4096]{0:T(1024)} %param.13) | copy-start | bytes 49156
  33.4 37.4 %copy-start.4 = (f32[256]{0:T(256)S(1)}, f32[256]{0:T(256)}, u32[]{:S(2)}) copy-start(f32[256]{0:T(256)} %param.11) | copy-start | bytes 3076
  72.9 19.1 %all-to-all-start.2 = ((bf16[16,128,128]{2,1,0:T(8,128)(2,1)}), bf16[16,128,128]{2,1,0:T(8,128)(2,1)S(1)}, u32[]{:S(2)}, u32[]{:S(2)}) async-start(bf16[16,128,128]{2,1,0:T(8,128)(2,1)} %get-tuple-element.29), calls=%async_computation.2 | async-start | bytes 1048576 | tf_op jit(solution)/shard_map/all_to_all | solution.py:31
  76.5 4.1 %collective-permute-start.3 = (f32[4,40,128]{2,1,0:T(8,128)S(1)}, f32[4,40,128]{2,1,0:T(8,128)S(1)}, u32[]{:S(2)}, u32[]{:S(2)}) collective-permute-start(f32[4,40,128]{2,1,0:T(8,128)S(1)} %get-tuple-element.34), channel_id=1, source_target_pairs={{0,16},{16,0},{32,48},{48,32},{64,80},{80,64},{96,112},{112,96},{1... | collective-permute-start | bytes 245768 | tf_op jit(solution)/shard_map/ppermute | solution.py:37
  79.1 6.4 %collective-permute-start.5 = (f32[4,40,128]{2,1,0:T(8,128)S(1)}, f32[4,40,128]{2,1,0:T(8,128)S(1)}, u32[]{:S(2)}, u32[]{:S(2)}) collective-permute-start(f32[4,40,128]{2,1,0:T(8,128)S(1)} %get-tuple-element.35), channel_id=1, source_target_pairs={{0,48},{16,32},{32,16},{48,0},{64,112},{80,96},{96,80},{112,64},{1... | collective-permute-start | bytes 245768 | tf_op jit(solution)/shard_map/ppermute | solution.py:37
  79.2 6.9 %collective-permute-start.4 = (f32[4,40,128]{2,1,0:T(8,128)S(1)}, f32[4,40,128]{2,1,0:T(8,128)S(1)}, u32[]{:S(2)}, u32[]{:S(2)}) collective-permute-start(f32[4,40,128]{2,1,0:T(8,128)S(1)} %get-tuple-element.35), channel_id=1, source_target_pairs={{0,32},{16,48},{32,0},{48,16},{64,96},{80,112},{96,64},{112,80},{1... | collective-permute-start | bytes 245768 | tf_op jit(solution)/shard_map/ppermute | solution.py:37
  86.2 18.6 %collective-permute-start.6 = (f32[40,128]{1,0:T(8,128)S(1)}, f32[40,128]{1,0:T(8,128)S(1)}, u32[]{:S(2)}, u32[]{:S(2)}) collective-permute-start(f32[40,128]{1,0:T(8,128)S(1)} %get-tuple-element.36), channel_id=1, source_target_pairs={{0,64},{16,80},{32,96},{48,112},{64,0},{80,16},{96,32},{112,48},{1... | collective-permute-start | bytes 61448 | tf_op jit(solution)/shard_map/ppermute | solution.py:37
  86.6 18.2 %collective-permute-start.8 = (f32[40,128]{1,0:T(8,128)S(1)}, f32[40,128]{1,0:T(8,128)S(1)}, u32[]{:S(2)}, u32[]{:S(2)}) collective-permute-start(f32[40,128]{1,0:T(8,128)S(1)} %get-tuple-element.37), channel_id=1, source_target_pairs={{0,192},{16,208},{32,224},{48,240},{64,128},{80,144},{96,160},{112... | collective-permute-start | bytes 61448 | tf_op jit(solution)/shard_map/ppermute | solution.py:37
  87.6 17.2 %collective-permute-start.7 = (f32[40,128]{1,0:T(8,128)S(1)}, f32[40,128]{1,0:T(8,128)S(1)}, u32[]{:S(2)}, u32[]{:S(2)}) collective-permute-start(f32[40,128]{1,0:T(8,128)S(1)} %get-tuple-element.38), channel_id=1, source_target_pairs={{0,128},{16,144},{32,160},{48,176},{64,192},{80,208},{96,224},{112... | collective-permute-start | bytes 61448 | tf_op jit(solution)/shard_map/ppermute | solution.py:37
  99.9 27.6 %collective-permute-start.2 = (bf16[16,128,128]{2,1,0:T(8,128)(2,1)S(1)}, bf16[16,128,128]{2,1,0:T(8,128)(2,1)S(1)}, u32[]{:S(2)}, u32[]{:S(2)}) collective-permute-start(bf16[16,128,128]{2,1,0:T(8,128)(2,1)S(1)} %spread_rest.1), channel_id=1, source_target_pairs={{0,16},{16,0},{32,48},{48,32},{64,80},{80,64},{96,112},{112,96},{1... | collective-permute-start | bytes 1572872 | tf_op jit(solution)/shard_map/ppermute | solution.py:37
  104.8 5.7 %collective-permute-start.11 = (f32[40,128]{1,0:T(8,128)S(1)}, f32[40,128]{1,0:T(8,128)S(1)}, u32[]{:S(2)}, u32[]{:S(2)}) collective-permute-start(f32[40,128]{1,0:T(8,128)S(1)} %fusion.2), channel_id=1, source_target_pairs={{0,12},{1,13},{2,14},{3,15},{4,8},{5,9},{6,10},{7,11},{8,4},{9,5},... | collective-permute-start | bytes 61448 | tf_op jit(solution)/shard_map/ppermute | solution.py:37
  105.2 6.7 %collective-permute-start.10 = (f32[40,128]{1,0:T(8,128)S(1)}, f32[40,128]{1,0:T(8,128)S(1)}, u32[]{:S(2)}, u32[]{:S(2)}) collective-permute-start(f32[40,128]{1,0:T(8,128)S(1)} %fusion.2), channel_id=1, source_target_pairs={{0,8},{1,9},{2,10},{3,11},{4,12},{5,13},{6,14},{7,15},{8,0},{9,1},... | collective-permute-start | bytes 61448 | tf_op jit(solution)/shard_map/ppermute | solution.py:37
  108.5 4.3 %collective-permute-start.9 = (f32[40,128]{1,0:T(8,128)S(1)}, f32[40,128]{1,0:T(8,128)S(1)}, u32[]{:S(2)}, u32[]{:S(2)}) collective-permute-start(f32[40,128]{1,0:T(8,128)S(1)} %fusion.2), channel_id=1, source_target_pairs={{0,4},{1,5},{2,6},{3,7},{4,0},{5,1},{6,2},{7,3},{8,12},{9,13},{10,... | collective-permute-start | bytes 61448 | tf_op jit(solution)/shard_map/ppermute | solution.py:37
  112.8 5.1 %collective-permute-start.14 = (f32[40,128]{1,0:T(8,128)S(1)}, f32[40,128]{1,0:T(8,128)S(1)}, u32[]{:S(2)}, u32[]{:S(2)}) collective-permute-start(f32[40,128]{1,0:T(8,128)S(1)} %add_add_fusion.2), channel_id=1, source_target_pairs={{0,3},{1,2},{2,1},{3,0},{4,7},{5,6},{6,5},{7,4},{8,11},{9,10},{10,... | collective-permute-start | bytes 61448 | tf_op jit(solution)/shard_map/ppermute | solution.py:37
  114.9 3.0 %collective-permute-start.13 = (f32[40,128]{1,0:T(8,128)S(1)}, f32[40,128]{1,0:T(8,128)S(1)}, u32[]{:S(2)}, u32[]{:S(2)}) collective-permute-start(f32[40,128]{1,0:T(8,128)S(1)} %add_add_fusion.2), channel_id=1, source_target_pairs={{0,2},{1,3},{2,0},{3,1},{4,6},{5,7},{6,4},{7,5},{8,10},{9,11},{10,... | collective-permute-start | bytes 61448 | tf_op jit(solution)/shard_map/ppermute | solution.py:37
  115.1 4.4 %collective-permute-start.12 = (f32[40,128]{1,0:T(8,128)S(1)}, f32[40,128]{1,0:T(8,128)S(1)}, u32[]{:S(2)}, u32[]{:S(2)}) collective-permute-start(f32[40,128]{1,0:T(8,128)S(1)} %add_add_fusion.2), channel_id=1, source_target_pairs={{0,1},{1,0},{2,3},{3,2},{4,5},{5,4},{6,7},{7,6},{8,9},{9,8},{10,11... | collective-permute-start | bytes 61448 | tf_op jit(solution)/shard_map/ppermute | solution.py:37
  129.0 12.9 %all-to-all-start.3 = ((bf16[16,160,128]{2,1,0:T(8,128)(2,1)}), bf16[16,160,128]{2,1,0:T(8,128)(2,1)S(1)}, u32[]{:S(2)}, u32[]{:S(2)}) async-start(bf16[16,160,128]{2,1,0:T(8,128)(2,1)} %join.1), calls=%async_computation.3 | async-start | bytes 1310720 | tf_op jit(solution)/shard_map/all_to_all | solution.py:31
